TPU v7x, 32 devices: a whole 2x2x4 slice. The times are simulated.
32 devices in a mesh: section: 2 (over y), expert: 4 (over z), dp: 4 (over x, core).
Axes of the slice: x: 2, y: 2, z: 4, core: 2. Of those that a mesh axis runs over, the one named last changes fastest.
Arguments:
- residual: bfloat16 [4096, 2048], P(('section', 'expert', 'dp')), may hold values from -12 to 12
- queries: bfloat16 [4096, 1024], P(('section', 'expert', 'dp')), may hold values from -6 to 6
- attn_keys: bfloat16 [4096, 1024], P(('section', 'expert', 'dp')), may hold values from -6 to 6
- attn_values: bfloat16 [4096, 1024], P(('section', 'expert', 'dp')), may hold values from -6 to 6
- out_weight: bfloat16 [1024, 2048], P('expert'), may hold values from -0.1875 to 0.1875
- norm_gain: float32 [2048], replicated, may hold values from 0.25 to 1.75
- gate_weight: bfloat16 [4, 2048, 4096], P('expert', None, 'dp'), may hold values from -0.125 to 0.125
- up_weight: bfloat16 [4, 2048, 4096], P('expert', None, 'dp'), may hold values from -0.125 to 0.125
- down_weight: bfloat16 [4, 4096, 2048], P('expert', 'dp'), may hold values from -0.09375 to 0.09375
- expert_ids: int32 [4096, 1], P(('section', 'expert', 'dp')), may hold values from 0 to 3; in each aligned block of 128 rows (0 to 127, 128 to 255, ...) at most 64 rows name the same one
- out_grad: bfloat16 [4096, 2048], P(('section', 'expert', 'dp')), may hold values from -6 to 6
Outputs:
- layer_out: bfloat16 [4096, 2048], P(('section', 'expert', 'dp'))
- resid_grad: bfloat16 [4096, 2048], P(('section', 'expert', 'dp'))
- query_grad: bfloat16 [4096, 1024], P(('section', 'expert', 'dp'))
- key_grad: bfloat16 [4096, 1024], P(('section', 'expert', 'dp'))
- value_grad: bfloat16 [4096, 1024], P(('section', 'expert', 'dp'))
- weight_grad: float32 [1024, 2048], P('expert')
Inputs may be any that keep to these rules, and one draw needn't show every extreme that they name: `expert_ids`: no expert is named by more than 64 of the 128 rows of one device (an aligned block); in every draw some block names one expert exactly 64 times.
All inputs are finite; a program needn't handle non-finite values.
Results may differ from a plain program's by a relative error of at most 0.023.
Values may be sent and summed in bfloat16 or wider, within the bound.
A program may use at most 128 MiB of HBM per device.

v0:
```python
import math

import jax
import jax.numpy as jnp
from jax import lax
from jax.sharding import PartitionSpec as P

D = 2048
HEADS = 8
HEAD = 128
A = 1024
FF = 4096


epsilon = 1e-06


def contract_last(left_side, right_side):
    return lax.dot_general(
        left_side, right_side, (((1,), (1,)), ((), ())), preferred_element_type=jnp.float32
    )


def contract_first(left_side, right_side):
    return lax.dot_general(
        left_side, right_side, (((0,), (0,)), ((), ())), preferred_element_type=jnp.float32
    )


def shards(
    residual,
    queries,
    attn_keys,
    attn_values,
    out_weight,
    norm_gain,
    gate_weight,
    up_weight,
    down_weight,
    expert_ids,
    out_grad,
):
    tokens_here = residual.shape[0]
    experts = lax.axis_size("expert")
    data_ways = lax.axis_size("dp")
    capacity = max(tokens_here // 8, 2 * tokens_here // experts)
    inv_root = 1.0 / math.sqrt(HEAD)
    keys_all, values_all = (
        lax.all_gather(attn_keys, "dp", axis=0, tiled=True),
        lax.all_gather(attn_values, "dp", axis=0, tiled=True),
    )
    query_heads = queries.reshape(tokens_here, HEADS, HEAD)
    key_heads = keys_all.reshape(-1, HEADS, HEAD)
    value_heads = values_all.reshape(-1, HEADS, HEAD)
    scores = (
        jnp.einsum("thd,shd->hts", query_heads, key_heads, preferred_element_type=jnp.float32)
        * inv_root
    )
    row_peak = jnp.max(scores, axis=-1, keepdims=True)
    exp_scores = jnp.exp(scores - row_peak)
    attn_probs = exp_scores / jnp.sum(exp_scores, axis=-1, keepdims=True)
    probs_low = attn_probs.astype(jnp.bfloat16)
    attended = (
        jnp.einsum("hts,shd->thd", probs_low, value_heads, preferred_element_type=jnp.float32)
        .reshape(tokens_here, A)
        .astype(jnp.bfloat16)
    )
    full_out = lax.all_gather(out_weight, "expert", axis=0, tiled=True)
    hidden = residual.astype(jnp.float32) + jnp.dot(
        attended, full_out, preferred_element_type=jnp.float32
    )
    inv_rms = lax.rsqrt(jnp.mean(hidden * hidden, axis=-1, keepdims=True) + epsilon)
    unit_rows = hidden * inv_rms
    normed = (unit_rows * norm_gain).astype(jnp.bfloat16)
    expert_of = expert_ids[:, 0]
    onehot = (expert_of[:, None] == jnp.arange(experts, dtype=jnp.int32)[None, :]).astype(
        jnp.bfloat16
    )
    row_iota = jnp.arange(tokens_here, dtype=jnp.int32)
    earlier_mask = (row_iota[:, None] > row_iota[None, :]).astype(jnp.bfloat16)
    earlier = jnp.dot(earlier_mask, onehot, preferred_element_type=jnp.float32)
    rank_index = jnp.sum(earlier * onehot.astype(jnp.float32), axis=1).astype(jnp.int32)
    slot_index = expert_of * capacity + rank_index
    empty_rows = jnp.zeros((experts * capacity, D), jnp.bfloat16)
    send_buffer = empty_rows.at[slot_index].set(normed).reshape(experts, capacity, D)
    gate_local = gate_weight[0]
    up_local = up_weight[0]
    down_local = down_weight[0]
    block_width = FF // data_ways
    arrived = lax.all_to_all(send_buffer, "expert", split_axis=0, concat_axis=0, tiled=True)
    piece_rows = arrived.shape[1]
    gathered = lax.all_gather(arrived, "dp", axis=0, tiled=True)
    flattened = gathered.reshape(-1, D)
    gate_pre = jnp.dot(flattened, gate_local, preferred_element_type=jnp.float32)
    up_pre = jnp.dot(flattened, up_local, preferred_element_type=jnp.float32)
    activated = (jax.nn.silu(gate_pre) * up_pre).astype(jnp.bfloat16)
    partial_out = jnp.dot(activated, down_local, preferred_element_type=jnp.float32)
    summed = lax.psum_scatter(
        partial_out.reshape(data_ways * experts, piece_rows, D).astype(jnp.bfloat16),
        "dp",
        scatter_dimension=0,
        tiled=True,
    )
    returned = lax.all_to_all(summed, "expert", split_axis=0, concat_axis=0, tiled=True)
    gate_saved = gate_pre.reshape(data_ways * experts, piece_rows, block_width)
    up_saved = up_pre.reshape(data_ways * experts, piece_rows, block_width)
    expert_back = returned.reshape(experts * capacity, D)[slot_index]
    layer_out = (hidden + expert_back.astype(jnp.float32)).astype(jnp.bfloat16)
    grad_buffer = empty_rows.at[slot_index].set(out_grad).reshape(experts, capacity, D)
    grad_arrived = lax.all_to_all(grad_buffer, "expert", split_axis=0, concat_axis=0, tiled=True)
    grad_gathered = lax.all_gather(grad_arrived, "dp", axis=0, tiled=True)
    grad_flat = grad_gathered.reshape(-1, D)
    gate_pre = gate_saved.reshape(-1, block_width)
    up_pre = up_saved.reshape(-1, block_width)
    sigmoid_gate = jax.nn.sigmoid(gate_pre)
    grad_act = contract_last(grad_flat, down_local)
    grad_gate = (grad_act * up_pre * sigmoid_gate * (1.0 + gate_pre * (1.0 - sigmoid_gate))).astype(
        jnp.bfloat16
    )
    grad_up = (grad_act * jax.nn.silu(gate_pre)).astype(jnp.bfloat16)
    partial_grad = contract_last(grad_gate, gate_local) + contract_last(grad_up, up_local)
    grad_normed_rows = lax.psum_scatter(
        partial_grad.reshape(data_ways * experts, capacity, D).astype(jnp.bfloat16),
        "dp",
        scatter_dimension=0,
        tiled=True,
    )
    grad_returned = lax.all_to_all(
        grad_normed_rows, "expert", split_axis=0, concat_axis=0, tiled=True
    )
    grad_normed = grad_returned.reshape(experts * capacity, D)[slot_index].astype(jnp.float32)
    scaled = grad_normed * norm_gain
    resid_grad = (
        out_grad.astype(jnp.float32)
        + inv_rms * (scaled - unit_rows * jnp.mean(scaled * unit_rows, axis=-1, keepdims=True))
    ).astype(jnp.bfloat16)
    grad_shard = lax.psum_scatter(
        contract_first(attended, resid_grad).astype(jnp.bfloat16),
        "expert",
        scatter_dimension=0,
        tiled=True,
    )
    weight_grad = lax.psum(grad_shard, ("section", "dp")).astype(jnp.float32)
    grad_attended = contract_last(resid_grad, full_out).astype(jnp.bfloat16)
    grad_heads = grad_attended.reshape(tokens_here, HEADS, HEAD)
    grad_probs = jnp.einsum(
        "thd,shd->hts", grad_heads, value_heads, preferred_element_type=jnp.float32
    )
    row_delta = jnp.sum(attn_probs * grad_probs, axis=-1, keepdims=True)
    grad_scores = (attn_probs * (grad_probs - row_delta)).astype(jnp.bfloat16)
    query_grad = (
        (
            jnp.einsum("hts,shd->thd", grad_scores, key_heads, preferred_element_type=jnp.float32)
            * inv_root
        )
        .reshape(tokens_here, A)
        .astype(jnp.bfloat16)
    )
    key_part = (
        jnp.einsum("hts,thd->shd", grad_scores, query_heads, preferred_element_type=jnp.float32)
        * inv_root
    )
    value_part = jnp.einsum(
        "hts,thd->shd", probs_low, grad_heads, preferred_element_type=jnp.float32
    )
    key_value = lax.psum_scatter(
        jnp.concatenate(
            [
                key_part.reshape(lax.axis_size("dp") * tokens_here, A),
                value_part.reshape(lax.axis_size("dp") * tokens_here, A),
            ],
            axis=1,
        ).astype(jnp.bfloat16),
        "dp",
        scatter_dimension=0,
        tiled=True,
    ).astype(jnp.float32)
    key_grad = key_value[:, :A].astype(jnp.bfloat16)
    value_grad = key_value[:, A:].astype(jnp.bfloat16)
    return (layer_out, resid_grad, query_grad, key_grad, value_grad, weight_grad)


def solution(mesh):
    return jax.shard_map(
        shards,
        mesh=mesh,
        in_specs=(
            P(("section", "expert", "dp"), None),
            P(("section", "expert", "dp"), None),
            P(("section", "expert", "dp"), None),
            P(("section", "expert", "dp"), None),
            P("expert", None),
            P(),
            P("expert", None, "dp"),
            P("expert", None, "dp"),
            P("expert", "dp", None),
            P(("section", "expert", "dp"), None),
            P(("section", "expert", "dp"), None),
        ),
        out_specs=(
            P(("section", "expert", "dp"), None),
            P(("section", "expert", "dp"), None),
            P(("section", "expert", "dp"), None),
            P(("section", "expert", "dp"), None),
            P(("section", "expert", "dp"), None),
            P("expert", None),
        ),
        check_vma=False,
    )
```

profile of v0, /device:TPU:0, one launch (start us, length us, event | category | flops | bytes accessed | tf_op | source)
XLA Modules:
  0.0 544.3 jit_solution(3329325886076428349)
XLA Ops:
  7.2 0.7 all-gather.8.cloned.1.call-update
  7.9 1.8 copy.38
  9.8 0.7 all-gather.10.cloned.1.call-update
  10.5 1.1 copy.51
  11.7 0.9 fusion.22
  12.6 0.7 fusion.37
  13.2 15.7 %all-gather.8.cloned.1.call-done = bf16[512,1024]{1,0:T(8,128)(2,1)} async-done(((bf16[128,1024]{1,0:T(8,128)(2,1)}), bf16[512,1024]{1,0:T(8,128)(2,1)}) %all-gather.8.cloned.1.call-update) | async-done | bytes 1048592 | tf_op jit(solution)/shard_map/all_gather | solution.py:50
  29.0 1.5 copy.41
  30.5 17.5 %all-gather.6.cloned.1.call-done = bf16[512,1024]{0,1:T(8,128)(2,1)} async-done(((bf16[128,1024]{0,1:T(8,128)(2,1)}), bf16[512,1024]{0,1:T(8,128)(2,1)}) %all-gather.6.cloned.1.call-update) | async-done | bytes 1048592 | tf_op jit(solution)/shard_map/all_gather | solution.py:49
  48.0 2.1 fusion.42
  50.1 1.4 convolution_convert_fusion.2
  51.5 78.8 %all-gather.10.cloned.1.call-done = bf16[1024,2048]{1,0:T(8,128)(2,1)} async-done(((bf16[256,2048]{1,0:T(8,128)(2,1)}), bf16[1024,2048]{1,0:T(8,128)(2,1)}) %all-gather.10.cloned.1.call-update) | async-done | bytes 4194320 | tf_op jit(solution)/shard_map/all_gather | solution.py:68
  130.3 3.2 multiply_reduce_fusion.3
  133.5 1.8 scatter_custom_fusion
  135.3 29.0 %all_to_all.20 = bf16[4,64,2048]{2,1,0:T(8,128)(2,1)} all-to-all(bf16[4,64,2048]{2,1,0:T(8,128)(2,1)S(1)} %bitcast.80), channel_id=1, replica_groups=mesh['section'=2,'expert'=4,'dp'=4] {'expert'}, dimensions={0} | all-to-all | bytes 2097152 | tf_op jit(solution)/shard_map/all_to_all | solution.py:90
  164.4 2.2 scatter_custom_fusion.1
  166.6 28.4 %all_to_all.21 = bf16[4,64,2048]{2,1,0:T(8,128)(2,1)} all-to-all(bf16[4,64,2048]{2,1,0:T(8,128)(2,1)S(1)} %bitcast.78), channel_id=1, replica_groups=mesh['section'=2,'expert'=4,'dp'=4] {'expert'}, dimensions={0} | all-to-all | bytes 2097152 | tf_op jit(solution)/shard_map/all_to_all | solution.py:110
  195.1 2.9 all-gather.12.cloned.1.call-done
  198.0 7.6 %fusion.11 = f32[1024,1024]{1,0:T(8,128)S(1)} fusion(bf16[1024,2048]{1,0:T(8,128)(2,1)} %bitcast.94, bf16[1,2048,1024]{2,1,0:T(8,128)(2,1)} %param.17), kind=kOutput, calls=%fused_computation.16 | convolution fusion | flops 4294967296 | bytes 12582912 | tf_op jit(solution)/shard_map/dot_general | solution.py:94
  205.7 6.5 %multiply_convert_fusion.2 = (bf16[1024,1024]{1,0:T(8,128)(2,1)S(1)}, f32[1024,1024]{1,0:T(8,128)}) fusion(f32[1024,1024]{1,0:T(8,128)S(1)} %fusion.11, bf16[1024,2048]{1,0:T(8,128)(2,1)S(1)} %bitcast.95, bf16[1,2048,1024]{2,1,0:T(8,128)(2,1)S(1)} %copy-done.10), kind=kOutput, calls=%fused_computation.20 | convolution fusion | flops 4301258752 | bytes 18874368 | tf_op jit(solution)/shard_map/dot_general | solution.py:95
  212.2 6.1 %fusion.14 = bf16[16,64,2048]{2,1,0:T(8,128)(2,1)} fusion(bf16[16,64,1024]{2,1,0:T(8,128)(2,1)S(1)} %bitcast.97, bf16[1,1024,2048]{2,1,0:T(8,128)(2,1)S(1)} %copy-done.9), kind=kOutput, calls=%fused_computation.24 | convolution fusion | flops 4297064448 | bytes 10485760 | tf_op jit(solution)/shard_map/dot_general | solution.py:97
  218.6 15.3 %all-gather.14.cloned.1.call-done = bf16[16,64,2048]{2,1,0:T(8,128)(2,1)} async-done(((bf16[4,64,2048]{2,1,0:T(8,128)(2,1)}), bf16[16,64,2048]{2,1,0:T(8,128)(2,1)}) %all-gather.14.cloned.1.call-update) | async-done | bytes 4194320 | tf_op jit(solution)/shard_map/all_gather | solution.py:111
  233.9 7.7 %fusion.3 = f32[1024,1024]{1,0:T(8,128)S(1)} fusion(bf16[1024,2048]{1,0:T(8,128)(2,1)} %bitcast.93, bf16[1,1024,2048]{2,1,0:T(8,128)(2,1)} %param.19), kind=kOutput, calls=%fused_computation.8 | convolution fusion | flops 4294967296 | bytes 12582912 | tf_op jit(solution)/shard_map/dot_general | solution.py:19
  241.7 6.9 %fusion.5 = f32[1024,2048]{1,0:T(8,128)} fusion(bf16[1,2048,1024]{2,1,0:T(8,128)(2,1)S(1)} %copy-done.11, f32[1024,1024]{1,0:T(8,128)S(1)} %fusion.3, f32[1024,1024]{1,0:T(8,128)S(1)} %copy-done.15), kind=kOutput, calls=%fused_computation.10 | convolution fusion | flops 4301258752 | bytes 20971520 | tf_op jit(solution)/shard_map/dot_general | solution.py:19
  248.5 14.3 %add_convert_fusion = bf16[1024,2048]{1,0:T(8,128)(2,1)} fusion(f32[1024,2048]{1,0:T(8,128)} %fusion.5, bf16[1,2048,1024]{2,1,0:T(8,128)(2,1)S(1)} %copy-done.12, f32[1024,1024]{1,0:T(8,128)} %copy-done.14, f32[1024,1024]{1,0:T(8,128)} %copy-done.16, f32[1024,1024]{1,0:T(8,128)} %get-tuple-element.33), kind=kOutput, calls=%fused_computation.5 | convolution fusion | flops 4309647360 | bytes 29360128 | tf_op jit(solution)/shard_map/dot_general | solution.py:19
  262.9 18.0 %reduce-scatter.5.cloned.1.call-done = bf16[4,64,2048]{2,1,0:T(8,128)(2,1)} async-done(((bf16[16,64,2048]{2,1,0:T(8,128)(2,1)}), bf16[4,64,2048]{2,1,0:T(8,128)(2,1)}) %reduce-scatter.5.cloned.1.call-update) | async-done | bytes 1048592 | tf_op jit(solution)/shard_map/reduce_scatter | solution.py:98
  280.9 4.6 all-to-all-start.1
  285.5 42.6 %reduce-scatter.7.cloned.1.call-done = bf16[4,64,2048]{2,1,0:T(8,128)(2,1)} async-done(((bf16[16,64,2048]{2,1,0:T(8,128)(2,1)}), bf16[4,64,2048]{2,1,0:T(8,128)(2,1)}) %reduce-scatter.7.cloned.1.call-update) | async-done | bytes 1048592 | tf_op jit(solution)/shard_map/reduce_scatter | solution.py:122
  328.1 4.6 all-to-all-start.3
  332.7 1.7 gather_fusion
  334.4 23.8 %all-to-all-done.3 = bf16[4,64,2048]{2,1,0:T(8,128)(2,1)S(1)} async-done(((bf16[4,64,2048]{2,1,0:T(8,128)(2,1)}), bf16[4,64,2048]{2,1,0:T(8,128)(2,1)S(1)}, u32[]{:S(2)}, u32[]{:S(2)}) %all-to-all-start.3) | async-done | bytes 1048608 | tf_op jit(solution)/shard_map/all_to_all | solution.py:128
  358.2 0.9 gather_fusion.1
  359.5 2.4 add_convert_fusion.1
  361.9 3.2 convolution_convert_fusion
  365.3 3.9 convolution_convert_fusion.3
  369.2 0.8 copy.52
  370.1 2.5 convolution_convert_fusion.1
  372.6 2.3 copy.47
  374.9 1.5 multiply_reduce_fusion
  377.2 1.3 copy.46
  378.5 2.8 pad_maximum_fusion
  381.5 58.7 %reduce-scatter.11.cloned.1.call-done = bf16[256,2048]{1,0:T(8,128)(2,1)} async-done(((bf16[1024,2048]{1,0:T(8,128)(2,1)}), bf16[256,2048]{1,0:T(8,128)(2,1)}) %reduce-scatter.11.cloned.1.call-update) | async-done | bytes 1048592 | tf_op jit(solution)/shard_map/reduce_scatter | solution.py:137
  440.2 0.4 fusion.21
  440.6 0.9 copy.48
  441.5 33.5 %reduce-scatter.9.cloned.1.call-done = bf16[128,2048]{1,0:T(8,128)(2,1)} async-done(((bf16[512,2048]{1,0:T(8,128)(2,1)}), bf16[128,2048]{1,0:T(8,128)(2,1)}) %reduce-scatter.9.cloned.1.call-update) | async-done | bytes 524304 | tf_op jit(solution)/shard_map/reduce_scatter | solution.py:166
  475.0 1.9 fusion.41
  476.8 57.9 %all-reduce.2.cloned.1.call-done = bf16[256,2048]{1,0:T(8,128)(2,1)} async-done(((bf16[256,2048]{1,0:T(8,128)(2,1)}), bf16[256,2048]{1,0:T(8,128)(2,1)}) %all-reduce.2.cloned.1.call-update) | async-done | bytes 1048592 | tf_op jit(solution)/shard_map/psum | solution.py:143
  534.7 2.8 convert_element_type.123
  (59 shorter events, 2.1 us)
Async XLA Ops:
  7.2 21.8 %all-gather.8.cloned.1.call-start = ((), (), s32[]{:S(2)}) async-start(), calls=%async_computation.9 | async-start | bytes 1310720 | tf_op jit(solution)/shard_map/all_gather | solution.py:50
  7.9 40.1 %all-gather.6.cloned.1.call-start = ((), (), s32[]{:S(2)}) async-start(), calls=%async_computation.8 | async-start | bytes 1310720 | tf_op jit(solution)/shard_map/all_gather | solution.py:49
  9.8 120.6 %all-gather.10.cloned.1.call-start = ((), (), s32[]{:S(2)}) async-start(), calls=%async_computation.10 | async-start | bytes 5242880 | tf_op jit(solution)/shard_map/all_gather | solution.py:68
  10.5 187.5 %all-gather.12.cloned.1.call-start = ((), (), s32[]{:S(2)}) async-start(), calls=%async_computation.11 | async-start | bytes 5242880 | tf_op jit(solution)/shard_map/all_gather | solution.py:92
  30.5 21.0 %copy-start.6 = (bf16[512,1024]{0,1:T(8,128)(2,1)}, bf16[512,1024]{0,1:T(8,128)(2,1)S(1)}, u32[]{:S(2)}) copy-start(bf16[512,1024]{0,1:T(8,128)(2,1)S(1)} %copy.41) | copy-start | bytes 3145732
  50.1 1.4 copy-start
  51.5 82.0 %copy-start.8 = (f32[2048]{0:T(1024)S(1)}, f32[2048]{0:T(1024)}, u32[]{:S(2)}) copy-start(f32[2048]{0:T(1024)} %param.16) | copy-start | bytes 24580
  164.4 69.5 %all-gather.14.cloned.1.call-start = ((), (), s32[]{:S(2)}) async-start(), calls=%async_computation.13 | async-start | bytes 5242880 | tf_op jit(solution)/shard_map/all_gather | solution.py:111
  195.1 85.8 %reduce-scatter.5.cloned.1.call-start = ((), (), s32[]{:S(2)}) async-start(), calls=%async_computation.12 | async-start | bytes 5242880 | tf_op jit(solution)/shard_map/reduce_scatter | solution.py:98
  198.0 7.7 %copy-start.10 = (bf16[1,2048,1024]{2,1,0:T(8,128)(2,1)S(1)}, bf16[1,2048,1024]{2,1,0:T(8,128)(2,1)}, u32[]{:S(2)}) copy-start(bf16[1,2048,1024]{2,1,0:T(8,128)(2,1)} %param.18) | copy-start | bytes 12582916
  198.0 7.7 %copy-start.13 = (bf16[16,64,2048]{2,1,0:T(8,128)(2,1)S(1)}, bf16[16,64,2048]{2,1,0:T(8,128)(2,1)}, u32[]{:S(2)}) copy-start(bf16[16,64,2048]{2,1,0:T(8,128)(2,1)} %all-gather.12.cloned.1.call-done) | copy-start | bytes 12582916
  205.7 6.6 %copy-start.14 = (f32[1024,1024]{1,0:T(8,128)}, f32[1024,1024]{1,0:T(8,128)S(1)}, u32[]{:S(2)}) copy-start(f32[1024,1024]{1,0:T(8,128)S(1)} %fusion.11) | copy-start | bytes 12582916
  205.7 6.6 %copy-start.9 = (bf16[1,1024,2048]{2,1,0:T(8,128)(2,1)S(1)}, bf16[1,1024,2048]{2,1,0:T(8,128)(2,1)}, u32[]{:S(2)}) copy-start(bf16[1,1024,2048]{2,1,0:T(8,128)(2,1)} %param.19) | copy-start | bytes 12582916
  218.4 109.7 %reduce-scatter.7.cloned.1.call-start = ((), (), s32[]{:S(2)}) async-start(), calls=%async_computation.14 | async-start | bytes 5242880 | tf_op jit(solution)/shard_map/reduce_scatter | solution.py:122
  233.9 7.7 %copy-start.11 = (bf16[1,2048,1024]{2,1,0:T(8,128)(2,1)S(1)}, bf16[1,2048,1024]{2,1,0:T(8,128)(2,1)}, u32[]{:S(2)}) copy-start(bf16[1,2048,1024]{2,1,0:T(8,128)(2,1)} %param.18) | copy-start | bytes 12582916
  233.9 7.7 %copy-start.15 = (f32[1024,1024]{1,0:T(8,128)S(1)}, f32[1024,1024]{1,0:T(8,128)}, u32[]{:S(2)}) copy-start(f32[1024,1024]{1,0:T(8,128)} %copy-done.14) | copy-start | bytes 12582916
  241.7 6.9 %copy-start.16 = (f32[1024,1024]{1,0:T(8,128)}, f32[1024,1024]{1,0:T(8,128)S(1)}, u32[]{:S(2)}) copy-start(f32[1024,1024]{1,0:T(8,128)S(1)} %fusion.3) | copy-start | bytes 12582916
  241.7 6.9 %copy-start.12 = (bf16[1,2048,1024]{2,1,0:T(8,128)(2,1)S(1)}, bf16[1,2048,1024]{2,1,0:T(8,128)(2,1)}, u32[]{:S(2)}) copy-start(bf16[1,2048,1024]{2,1,0:T(8,128)(2,1)} %param.17) | copy-start | bytes 12582916
  280.9 47.2 %all-to-all-start.1 = ((bf16[4,64,2048]{2,1,0:T(8,128)(2,1)}), bf16[4,64,2048]{2,1,0:T(8,128)(2,1)S(1)}, u32[]{:S(2)}, u32[]{:S(2)}) async-start(bf16[4,64,2048]{2,1,0:T(8,128)(2,1)} %reduce-scatter.5.cloned.1.call-done), calls=%async_computation.2 | async-start | bytes 2097152 | tf_op jit(solution)/shard_map/all_to_all | solution.py:104
  328.1 30.1 %all-to-all-start.3 = ((bf16[4,64,2048]{2,1,0:T(8,128)(2,1)}), bf16[4,64,2048]{2,1,0:T(8,128)(2,1)S(1)}, u32[]{:S(2)}, u32[]{:S(2)}) async-start(bf16[4,64,2048]{2,1,0:T(8,128)(2,1)} %reduce-scatter.7.cloned.1.call-done), calls=%async_computation.5 | async-start | bytes 2097152 | tf_op jit(solution)/shard_map/all_to_all | solution.py:128
  332.7 107.5 %reduce-scatter.11.cloned.1.call-start = ((), (), s32[]{:S(2)}) async-start(), calls=%async_computation.16 | async-start | bytes 5242880 | tf_op jit(solution)/shard_map/reduce_scatter | solution.py:137
  359.2 2.7 copy-start.5
  361.9 3.5 copy-start.2
  365.0 5.0 copy-start.1
  365.1 109.9 %reduce-scatter.9.cloned.1.call-start = ((), (), s32[]{:S(2)}) async-start(), calls=%async_computation.15 | async-start | bytes 2621440 | tf_op jit(solution)/shard_map/reduce_scatter | solution.py:166
  370.1 4.8 copy-start.7
  376.8 1.8 copy-start.4
  378.5 61.6 %copy-start.3 = (bf16[512,1024]{0,1:T(8,128)(2,1)S(1)}, bf16[512,1024]{0,1:T(8,128)(2,1)}, u32[]{:S(2)}) copy-start(bf16[512,1024]{0,1:T(8,128)(2,1)} %all-gather.6.cloned.1.call-done) | copy-start | bytes 3145732
  381.4 153.3 %all-reduce.2.cloned.1.call-start = ((), (), s32[]{:S(2)}) async-start(), calls=%async_computation.17 | async-start | bytes 2097152 | tf_op jit(solution)/shard_map/psum | solution.py:143
Sparse Core Ops, SparseCore 0:
  9.5 19.4 all-gather.7
  31.1 16.8 all-gather.5
  49.5 80.7 all-gather.9
  164.5 33.4 all-gather.11
  199.4 34.4 all-gather.13
  236.3 44.5 reduce-scatter.4
  283.4 44.5 reduce-scatter.6
  365.2 74.9 reduce-scatter.10
  443.2 31.6 reduce-scatter.8
  478.0 56.6 all-reduce.1
where the time goes:
time: 545 us; the launch traced here: 544 us
  waiting for transfers between devices  366 us (67%)
  matrix products  68.7 us (13%)
  blocking collectives  57.4 us (11%)
  local copies, waits for them, and re-layouts  16.5 us (3%)
  between operations  14.4 us (3%)
  other arithmetic  11.2 us (2%)
  starting transfers between devices  9.97 us (2%)
    all_gather x1, waiting for transfers between devices, shards(): full_out = lax.all_gather(out_weight, 'expert', axis=0, tiled=True)  78.8 us
    reduce_scatter x1, waiting for transfers between devices, shards(): lax.psum_scatter(contract_first(attended, resid_grad).astype(jnp.bfloat16...  58.7 us
    psum x1, waiting for transfers between devices, shards(): weight_grad = lax.psum(grad_shard, ('section', 'dp')).astype(jnp.float32)  57.9 us
    reduce_scatter x1, waiting for transfers between devices, shards(): lax.psum_scatter(partial_grad.reshape(data_ways * experts, capacity, D).a...  42.6 us
    reduce_scatter x1, waiting for transfers between devices, shards(): lax.psum_scatter(jnp.concatenate([key_part.reshape(lax.axis_size('dp') *...  33.5 us
    dot_general x4, matrix products, contract_last(): lax.dot_general(left_side, right_side, (((1,), (1,)), ((), ())), preferre...  32.7 us
    all_to_all x1, blocking collectives, shards(): lax.all_to_all(send_buffer, 'expert', split_axis=0, concat_axis=0, tiled=...  29 us
    all_to_all x1, blocking collectives, shards(): lax.all_to_all(grad_buffer, 'expert', split_axis=0, concat_axis=0, tiled=...  28.4 us
  transfers between devices with their start and end apart: 12, of which 11 were waited for; matrix products, arithmetic and copies ran while one was open for 15% of the time, Pallas kernels for 0%

commit v1 on v0

v1 whole, which is shorter than its diff:
```python
import functools
import math

import jax
import jax.numpy as jnp
from jax import lax
from jax.experimental import pallas as pl
from jax.experimental.pallas import tpu as pltpu
from jax.sharding import PartitionSpec as P

D = 2048
HEADS = 8
HEAD = 128
A = 1024
FF = 4096


epsilon = 1e-06


def contract_last(left_side, right_side):
    return lax.dot_general(
        left_side, right_side, (((1,), (1,)), ((), ())), preferred_element_type=jnp.float32
    )


def contract_first(left_side, right_side):
    return lax.dot_general(
        left_side, right_side, (((0,), (0,)), ((), ())), preferred_element_type=jnp.float32
    )


MESH = pl.DeviceIdType.MESH
WHOLE = pl.BlockSpec(memory_space=pltpu.VMEM)


def flip(index, mask, size):
    total, bit = 0, 1
    while bit < size:
        here = lax.rem(lax.div(index, bit), 2)
        total = total + bit * ((1 - here) if (mask // bit) % 2 else here)
        bit *= 2
    return total


class Wire:
    def __init__(self, sizes, send_sems, recv_sems):
        self.sections, self.experts, self.ways = sizes
        self.outer = self.ways // 2
        self.section = lax.axis_index("section")
        self.expert = lax.axis_index("expert")
        self.dp = lax.axis_index("dp")
        self.low = lax.rem(self.dp, 2)
        self.high = lax.div(self.dp, 2)
        self.send_sems, self.recv_sems = send_sems, recv_sems
        self.started = []

    def send(self, source, target, peer):
        slot = len(self.started)
        copy = pltpu.make_async_remote_copy(
            src_ref=source,
            dst_ref=target,
            send_sem=self.send_sems.at[slot],
            recv_sem=self.recv_sems.at[slot],
            device_id=peer,
            device_id_type=MESH,
        )
        copy.start()
        self.started.append(copy)
        return copy

    def finish(self):
        for copy in self.started:
            copy.wait_send()

    def expert_at(self, mask):
        return flip(self.expert, mask, self.experts)

    def high_at(self, mask):
        return flip(self.high, mask, self.outer)

    def section_at(self, mask):
        return flip(self.section, mask, self.sections)

    def dp_at(self, mask):
        return self.high_at(mask) * 2 + self.low

    def to_expert(self, mask):
        return {"expert": self.expert_at(mask)}

    def to_high(self, mask):
        return {"dp": self.dp_at(mask)}

    def to_section(self, mask):
        return {"section": self.section_at(mask)}

    def to_low(self):
        return {"dp": self.high * 2 + (1 - self.low)}

    def expert_masks(self):
        half = self.experts // 2
        return list(range(half, self.experts)) + list(range(1, half))

    def greet(self, experts=True, sections=False):
        peers = [self.to_low()] + [self.to_high(m) for m in range(1, self.outer)]
        if experts:
            peers += [self.to_expert(m) for m in range(1, self.experts)]
        if sections:
            peers += [self.to_section(m) for m in range(1, self.sections)]
        barrier = pltpu.get_barrier_semaphore()
        for peer in peers:
            pl.semaphore_signal(barrier, inc=1, device_id=peer, device_id_type=MESH)
        pl.semaphore_wait(barrier, len(peers))


def added(first, *others):
    total = first.astype(jnp.float32)
    for other in others:
        total = total + other.astype(jnp.float32)
    return total.astype(jnp.bfloat16)


def gather_start(wire, block, out):
    wide = [wire.send(block, out.at[wire.dp], wire.to_high(m)) for m in range(1, wire.outer)]
    near = wire.send(block, out.at[wire.dp], wire.to_low())
    return wide, near


def gather_end(wire, flow, out):
    wide, near = flow
    passed = [near]
    for m, copy in enumerate(wide, 1):
        copy.wait_recv()
        block = out.at[wire.dp_at(m)]
        passed.append(wire.send(block, block, wire.to_low()))
    return passed


def cross(wire, source, out):
    return {
        m: wire.send(source.at[wire.expert_at(m)], out.at[wire.dp, wire.expert], wire.to_expert(m))
        for m in wire.expert_masks()
    }


def spread(wire, source, out, crossing):
    passed = []
    held = None

    def hand_over(mask, wide):
        for m, copy in enumerate(wide, 1):
            copy.wait_recv()
            block = out.at[wire.dp_at(m), wire.expert_at(mask)]
            passed.append(wire.send(block, block, wire.to_low()))

    for mask in [0] + wire.expert_masks():
        target = out.at[wire.dp, wire.expert_at(mask)]
        if mask:
            crossing[mask].wait_recv()
            block = target
        else:
            block = source.at[wire.expert]
        wide = [wire.send(block, target, wire.to_high(m)) for m in range(1, wire.outer)]
        passed.append(wire.send(block, target, wire.to_low()))
        if held is not None:
            hand_over(*held)
        held = (mask, wide)
    hand_over(*held)
    return passed


def settle(wire, passed):
    for copy in passed:
        copy.wait_recv()
    wire.finish()


def dispatch_kernel(sizes, rows, out, send_sems, recv_sems, own_sem):
    wire = Wire(sizes, send_sems, recv_sems)
    own = pltpu.make_async_copy(
        rows.at[wire.expert], out.at[wire.dp, wire.expert], own_sem
    )
    own.start()
    wire.greet()
    crossing = cross(wire, rows, out)
    passed = spread(wire, rows, out, crossing)
    settle(wire, passed)
    own.wait()


def opening_kernel(
    sizes, keys, values, weight, rows, keys_out, values_out, weight_out, out,
    send_sems, recv_sems, own_sems,
):
    wire = Wire(sizes, send_sems, recv_sems)
    local = [
        pltpu.make_async_copy(source, target, own_sems.at[i])
        for i, (source, target) in enumerate(
            (
                (keys, keys_out.at[wire.dp]),
                (values, values_out.at[wire.dp]),
                (weight, weight_out.at[wire.expert]),
                (rows.at[wire.expert], out.at[wire.dp, wire.expert]),
            )
        )
    ]
    for copy in local:
        copy.start()
    wire.greet(sections=True)
    key_flow = gather_start(wire, keys, keys_out)
    value_flow = gather_start(wire, values, values_out)
    part = wire.section * 2 + wire.low
    crossing = cross(wire, rows, out)
    quarters = {
        m: wire.send(weight.at[part], weight_out.at[wire.expert, part], wire.to_expert(m))
        for m in wire.expert_masks()
    }
    passed = gather_end(wire, key_flow, keys_out) + gather_end(wire, value_flow, values_out)
    passed += spread(wire, rows, out, crossing)
    sideways = {}
    for mask in wire.expert_masks():
        quarters[mask].wait_recv()
        block = weight_out.at[wire.expert_at(mask), part]
        sideways[mask] = [
            wire.send(block, block, wire.to_section(m)) for m in range(1, wire.sections)
        ]
        passed.append(wire.send(block, block, wire.to_low()))
    for mask in wire.expert_masks():
        for m, copy in enumerate(sideways[mask], 1):
            copy.wait_recv()
            block = weight_out.at[wire.expert_at(mask), wire.section_at(m) * 2 + wire.low]
            passed.append(wire.send(block, block, wire.to_low()))
    settle(wire, passed)
    for copy in local:
        copy.wait()


def fold_start(wire, parts, near_in, chunks):
    return {
        c: [
            wire.send(
                parts.at[h * 2 + (1 - wire.low), index],
                near_in.at[h, index],
                wire.to_low(),
            )
            for h in range(wire.outer)
        ]
        for c, index in chunks
    }


def fold_near(wire, flows, parts, near_in, far_in, c, index):
    for copy in flows[c]:
        copy.wait_recv()
    for h in range(wire.outer):
        near_in[h, index] = added(parts[h * 2 + wire.low, index], near_in[h, index])
    return [
        wire.send(near_in.at[wire.high_at(m), index], far_in.at[m - 1, index], wire.to_high(m))
        for m in range(1, wire.outer)
    ]


def fold_far(wire, far, near_in, far_in, index):
    for copy in far:
        copy.wait_recv()
    return added(
        near_in[wire.high, index], *[far_in[m - 1, index] for m in range(1, wire.outer)]
    )


def return_kernel(sizes, parts, out, near_in, far_in, total, send_sems, recv_sems):
    wire = Wire(sizes, send_sems, recv_sems)
    wire.greet()
    masks = wire.expert_masks() + [0]
    chunks = [(m, wire.expert_at(m)) for m in masks]
    flows = fold_start(wire, parts, near_in, chunks)
    far = {c: fold_near(wire, flows, parts, near_in, far_in, c, index) for c, index in chunks}
    arriving = []
    for c, index in chunks:
        summed = fold_far(wire, far[c], near_in, far_in, index)
        if c == 0:
            out[index] = summed
        else:
            total[index] = summed
            arriving.append(
                wire.send(total.at[index], out.at[wire.expert], wire.to_expert(c))
            )
    settle(wire, arriving)


def closing_kernel(
    sizes, parts, products, out, weight_out,
    near_in, far_in, low_in, side_in, high_in, total, cross_in, send_sems, recv_sems,
):
    wire = Wire(sizes, send_sems, recv_sems)
    wire.greet(sections=True)
    outer, sections = wire.outer, wire.sections
    span = outer * sections
    masks = wire.expert_masks() + [0]
    shards = [(m, wire.expert_at(m)) for m in masks]
    lows = {
        c: wire.send(
            products.at[pl.ds((1 - wire.low) * span, span), index],
            low_in.at[index],
            wire.to_low(),
        )
        for c, index in shards
    }
    pairs = [(i, i) for i in range(parts.shape[1])]
    flows = fold_start(wire, parts, near_in, pairs)
    sides = {}
    for c, index in shards:
        lows[c].wait_recv()
        for p in range(span):
            low_in[index, p] = added(products[wire.low * span + p, index], low_in[index, p])
        sides[c] = [
            wire.send(
                low_in.at[index, pl.ds(wire.section_at(m) * outer, outer)],
                side_in.at[m - 1, index],
                wire.to_section(m),
            )
            for m in range(1, sections)
        ]
    far = {c: fold_near(wire, flows, parts, near_in, far_in, c, index) for c, index in pairs}
    highs = {}
    for c, index in shards:
        for copy in sides[c]:
            copy.wait_recv()
        for h in range(outer):
            place = wire.section * outer + h
            low_in[index, place] = added(
                low_in[index, place], *[side_in[m - 1, index, h] for m in range(1, sections)]
            )
        highs[c] = [
            wire.send(
                low_in.at[index, wire.section * outer + wire.high_at(m)],
                high_in.at[m - 1, index],
                wire.to_high(m),
            )
            for m in range(1, outer)
        ]
    crossing = {}
    mine = None
    for c, index in shards:
        for copy in highs[c]:
            copy.wait_recv()
        summed = added(
            low_in[index, wire.section * outer + wire.high],
            *[high_in[m - 1, index] for m in range(1, outer)],
        )
        total[index] = summed
        if c:
            crossing[c] = wire.send(total.at[index], cross_in.at[c - 1], wire.to_expert(c))
    for c, index in pairs:
        out[index] = fold_far(wire, far[c], near_in, far_in, index)
    for c in crossing:
        crossing[c].wait_recv()
    place = wire.low * span + wire.section * outer + wire.high
    weight_out[place] = added(
        total[wire.expert], *[cross_in[m - 1] for m in range(1, wire.experts)]
    )
    base = wire.low * span
    passed = []
    wide = [
        wire.send(weight_out.at[place], weight_out.at[place], wire.to_high(m))
        for m in range(1, outer)
    ]
    side = [
        wire.send(weight_out.at[place], weight_out.at[place], wire.to_section(m))
        for m in range(1, sections)
    ]
    passed.append(wire.send(weight_out.at[place], weight_out.at[place], wire.to_low()))
    relayed = []
    for m, copy in enumerate(wide, 1):
        copy.wait_recv()
        block = weight_out.at[base + wire.section * outer + wire.high_at(m)]
        relayed += [
            (m, s, wire.send(block, block, wire.to_section(s))) for s in range(1, sections)
        ]
        passed.append(wire.send(block, block, wire.to_low()))
    for s, copy in enumerate(side, 1):
        copy.wait_recv()
        block = weight_out.at[base + wire.section_at(s) * outer + wire.high]
        passed.append(wire.send(block, block, wire.to_low()))
    for m, s, copy in relayed:
        copy.wait_recv()
        block = weight_out.at[base + wire.section_at(s) * outer + wire.high_at(m)]
        passed.append(wire.send(block, block, wire.to_low()))
    settle(wire, passed)


def call(kernel, sizes, ident, copies, operands, outs, scratch=(), extra=()):
    low = lambda shape: jax.ShapeDtypeStruct(shape, jnp.bfloat16)
    return pl.pallas_call(
        functools.partial(kernel, sizes),
        out_shape=[low(s) for s in outs],
        in_specs=[WHOLE] * len(operands),
        out_specs=[WHOLE] * len(outs),
        scratch_shapes=[pltpu.VMEM(s, jnp.bfloat16) for s in scratch]
        + [pltpu.SemaphoreType.DMA((copies,)), pltpu.SemaphoreType.DMA((copies,))]
        + list(extra),
        compiler_params=pltpu.CompilerParams(
            collective_id=ident, has_side_effects=True, vmem_limit_bytes=60 * 1024 * 1024
        ),
    )(*operands)


def shards(
    residual,
    queries,
    attn_keys,
    attn_values,
    out_weight,
    norm_gain,
    gate_weight,
    up_weight,
    down_weight,
    expert_ids,
    out_grad,
):
    tokens_here = residual.shape[0]
    experts = lax.axis_size("expert")
    data_ways = lax.axis_size("dp")
    capacity = max(tokens_here // 8, 2 * tokens_here // experts)
    inv_root = 1.0 / math.sqrt(HEAD)
    sections = lax.axis_size("section")
    sizes = (sections, experts, data_ways)
    outer = data_ways // 2
    expert_of = expert_ids[:, 0]
    onehot = (expert_of[:, None] == jnp.arange(experts, dtype=jnp.int32)[None, :]).astype(
        jnp.bfloat16
    )
    row_iota = jnp.arange(tokens_here, dtype=jnp.int32)
    earlier_mask = (row_iota[:, None] > row_iota[None, :]).astype(jnp.bfloat16)
    earlier = jnp.dot(earlier_mask, onehot, preferred_element_type=jnp.float32)
    rank_index = jnp.sum(earlier * onehot.astype(jnp.float32), axis=1).astype(jnp.int32)
    slot_index = expert_of * capacity + rank_index
    slot_iota = jnp.arange(experts * capacity, dtype=jnp.int32)
    placing = (slot_iota[:, None] == slot_index[None, :]).astype(jnp.bfloat16)
    buckets = (experts, capacity, D)
    spread_shape = (data_ways,) + buckets
    grad_buffer = jnp.dot(placing, out_grad).reshape(buckets)
    weight_rows = out_weight.shape[0]
    quarter = 2 * sections
    keys_all, values_all, full_out, grad_gathered = call(
        opening_kernel,
        sizes,
        0,
        4 * outer + experts * (1 + 2 * outer) + experts * (2 + 2 * sections),
        (
            attn_keys,
            attn_values,
            out_weight.reshape(quarter, weight_rows // quarter, D),
            grad_buffer,
        ),
        (
            (data_ways,) + attn_keys.shape,
            (data_ways,) + attn_values.shape,
            (experts, quarter, weight_rows // quarter, D),
            spread_shape,
        ),
        extra=(pltpu.SemaphoreType.DMA((4,)),),
    )
    full_out = full_out.reshape(A, D)
    query_heads = queries.reshape(tokens_here, HEADS, HEAD)
    key_heads = keys_all.reshape(-1, HEADS, HEAD)
    value_heads = values_all.reshape(-1, HEADS, HEAD)
    scores = (
        jnp.einsum("thd,shd->hts", query_heads, key_heads, preferred_element_type=jnp.float32)
        * inv_root
    )
    row_peak = jnp.max(scores, axis=-1, keepdims=True)
    exp_scores = jnp.exp(scores - row_peak)
    attn_probs = exp_scores / jnp.sum(exp_scores, axis=-1, keepdims=True)
    probs_low = attn_probs.astype(jnp.bfloat16)
    attended = (
        jnp.einsum("hts,shd->thd", probs_low, value_heads, preferred_element_type=jnp.float32)
        .reshape(tokens_here, A)
        .astype(jnp.bfloat16)
    )
    hidden = residual.astype(jnp.float32) + jnp.dot(
        attended, full_out, preferred_element_type=jnp.float32
    )
    inv_rms = lax.rsqrt(jnp.mean(hidden * hidden, axis=-1, keepdims=True) + epsilon)
    unit_rows = hidden * inv_rms
    normed = (unit_rows * norm_gain).astype(jnp.bfloat16)
    send_buffer = jnp.dot(placing, normed).reshape(buckets)
    gate_local = gate_weight[0]
    up_local = up_weight[0]
    down_local = down_weight[0]
    block_width = FF // data_ways
    (gathered,) = call(
        dispatch_kernel,
        sizes,
        1,
        experts * (1 + 2 * outer),
        (send_buffer,),
        (spread_shape,),
        extra=(pltpu.SemaphoreType.DMA,),
    )
    flattened = gathered.reshape(-1, D)
    gate_pre = jnp.dot(flattened, gate_local, preferred_element_type=jnp.float32)
    up_pre = jnp.dot(flattened, up_local, preferred_element_type=jnp.float32)
    activated = (jax.nn.silu(gate_pre) * up_pre).astype(jnp.bfloat16)
    partial_out = jnp.dot(activated, down_local, preferred_element_type=jnp.float32)
    back_copies = experts * (1 + outer + outer)
    back_scratch = ((outer,) + buckets, (max(outer - 1, 1),) + buckets, buckets)
    (returned,) = call(
        return_kernel,
        sizes,
        2,
        back_copies,
        (partial_out.astype(jnp.bfloat16).reshape(spread_shape),),
        (buckets,),
        back_scratch,
    )
    expert_back = contract_first(placing, returned.reshape(experts * capacity, D))
    layer_out = (hidden + expert_back.astype(jnp.float32)).astype(jnp.bfloat16)
    grad_flat = grad_gathered.reshape(-1, D)
    sigmoid_gate = jax.nn.sigmoid(gate_pre)
    grad_act = contract_last(grad_flat, down_local)
    grad_gate = (grad_act * up_pre * sigmoid_gate * (1.0 + gate_pre * (1.0 - sigmoid_gate))).astype(
        jnp.bfloat16
    )
    grad_up = (grad_act * jax.nn.silu(gate_pre)).astype(jnp.bfloat16)
    partial_grad = contract_last(grad_gate, gate_local) + contract_last(grad_up, up_local)
    (grad_returned,) = call(
        return_kernel,
        sizes,
        3,
        back_copies,
        (partial_grad.astype(jnp.bfloat16).reshape(spread_shape),),
        (buckets,),
        back_scratch,
    )
    grad_normed = contract_first(placing, grad_returned.reshape(experts * capacity, D))
    scaled = grad_normed * norm_gain
    resid_grad = (
        out_grad.astype(jnp.float32)
        + inv_rms * (scaled - unit_rows * jnp.mean(scaled * unit_rows, axis=-1, keepdims=True))
    ).astype(jnp.bfloat16)
    ways = data_ways * sections
    width = D // ways
    products = jnp.einsum(
        "ta,tpc->pac",
        attended,
        resid_grad.reshape(tokens_here, ways, width),
        preferred_element_type=jnp.float32,
    ).astype(jnp.bfloat16)
    grad_attended = contract_last(resid_grad, full_out).astype(jnp.bfloat16)
    grad_heads = grad_attended.reshape(tokens_here, HEADS, HEAD)
    grad_probs = jnp.einsum(
        "thd,shd->hts", grad_heads, value_heads, preferred_element_type=jnp.float32
    )
    row_delta = jnp.sum(attn_probs * grad_probs, axis=-1, keepdims=True)
    grad_scores = (attn_probs * (grad_probs - row_delta)).astype(jnp.bfloat16)
    query_grad = (
        (
            jnp.einsum("hts,shd->thd", grad_scores, key_heads, preferred_element_type=jnp.float32)
            * inv_root
        )
        .reshape(tokens_here, A)
        .astype(jnp.bfloat16)
    )
    key_part = (
        jnp.einsum("hts,thd->shd", grad_scores, query_heads, preferred_element_type=jnp.float32)
        * inv_root
    )
    value_part = jnp.einsum(
        "hts,thd->shd", probs_low, grad_heads, preferred_element_type=jnp.float32
    )
    pair_parts = jnp.stack(
        [
            key_part.reshape(data_ways, tokens_here, A),
            value_part.reshape(data_ways, tokens_here, A),
        ],
        axis=1,
    ).astype(jnp.bfloat16)
    pair = (2, tokens_here, A)
    block = (weight_rows, width)
    key_value, weight_parts = call(
        closing_kernel,
        sizes,
        4,
        4 * outer + experts * (1 + sections + outer + 1) + 3 * ways,
        (pair_parts, products.reshape(ways, experts, weight_rows, width)),
        (pair, (ways,) + block),
        (
            (outer,) + pair,
            (max(outer - 1, 1),) + pair,
            (experts, outer * sections) + block,
            (max(sections - 1, 1), experts, outer) + block,
            (max(outer - 1, 1), experts) + block,
            (experts,) + block,
            (experts - 1,) + block,
        ),
    )
    key_grad, value_grad = key_value[0], key_value[1]
    weight_grad = weight_parts.transpose(1, 0, 2).reshape(weight_rows, D).astype(jnp.float32)
    return (layer_out, resid_grad, query_grad, key_grad, value_grad, weight_grad)


def solution(mesh):
    return jax.shard_map(
        shards,
        mesh=mesh,
        in_specs=(
            P(("section", "expert", "dp"), None),
            P(("section", "expert", "dp"), None),
            P(("section", "expert", "dp"), None),
            P(("section", "expert", "dp"), None),
            P("expert", None),
            P(),
            P("expert", None, "dp"),
            P("expert", None, "dp"),
            P("expert", "dp", None),
            P(("section", "expert", "dp"), None),
            P(("section", "expert", "dp"), None),
        ),
        out_specs=(
            P(("section", "expert", "dp"), None),
            P(("section", "expert", "dp"), None),
            P(("section", "expert", "dp"), None),
            P(("section", "expert", "dp"), None),
            P(("section", "expert", "dp"), None),
            P("expert", None),
        ),
        check_vma=False,
    )
```

time: 545 us -> 377 us (0.69)
  waiting for transfers between devices: 366 us -> 0 us
  Pallas kernels: 0 us -> 255 us
  blocking collectives: 57.4 us -> 0 us
  matrix products: 68.7 us -> 83.1 us
  between operations: 14.4 us -> 1 us
  local copies, waits for them, and re-layouts: 16.5 us -> 27.7 us
  starting transfers between devices: 9.97 us -> 0 us
    pallas_call x0 -> x5, Pallas kernels: none -> 255 us  [call(): pl.pallas_call(functools.partial(kernel, sizes), out_shape=[low(s) for s...]
    reduce_scatter x4 -> x0, waiting for transfers between devices: 153 us -> none  [the longest x1 58.7 us: shards(): lax.psum_scatter(contract_first(attended, resid_grad).astype(jnp.bfloat16...]
    all_gather x5 -> x0, waiting for transfers between devices: 130 us -> none  [the longest x1 78.8 us: shards(): full_out = lax.all_gather(out_weight, 'expert', axis=0, tiled=True)]
    psum x1 -> x0, waiting for transfers between devices: 57.9 us -> none  [shards(): weight_grad = lax.psum(grad_shard, ('section', 'dp')).astype(jnp.float32)]
    all_to_all x2 -> x0, blocking collectives: 57.4 us -> none  [the longest x1 29 us: shards(): lax.all_to_all(send_buffer, 'expert', split_axis=0, concat_axis=0, tiled=...]
    all_to_all x2 -> x0, waiting for transfers between devices: 23.8 us -> none  [the longest x1 23.8 us: shards(): lax.all_to_all(grad_normed_rows, 'expert', split_axis=0, concat_axis=0, t...]
    convert_element_type x0 -> x2, local copies, waits for them, and re-layouts: none -> 9.39 us  [the longest x1 6.46 us: shards(): products = jnp.einsum('ta,tpc->pac', attended, resid_grad.reshape(tokens_...]
    all_to_all x2 -> x0, starting transfers between devices: 9.2 us -> none  [the longest x1 4.6 us: shards(): lax.all_to_all(grad_normed_rows, 'expert', split_axis=0, concat_axis=0, t...]
  transfers between devices with their start and end apart: 12 -> 0, of which waited for: 11 -> 0; matrix products, arithmetic and copies ran while one was open for 15% -> 0% of each run, Pallas kernels for 0% -> 0%
where the time goes in v1:
time: 377 us; the launch traced here: 376 us
  Pallas kernels  255 us (68%)
  matrix products  83.1 us (22%)
  local copies, waits for them, and re-layouts  27.7 us (7%)
  other arithmetic  8.98 us (2%)
    pallas_call x5, Pallas kernels, call(): pl.pallas_call(functools.partial(kernel, sizes), out_shape=[low(s) for s...  255 us
    dot_general x4, matrix products, contract_last(): lax.dot_general(left_side, right_side, (((1,), (1,)), ((), ())), preferre...  29.5 us
    dot_general x1, matrix products, shards(): jnp.dot(activated, down_local, preferred_element_type=jnp.float32)  11.1 us
    unnamed x40, local copies, waits for them, and re-layouts  8.57 us
    dot_general x1, matrix products, shards(): jnp.dot(flattened, gate_local, preferred_element_type=jnp.float32)  7.66 us

profile of v1, /device:TPU:0, one launch (start us, length us, event | category | flops | bytes accessed | tf_op | source)
XLA Modules:
  0.0 375.7 jit_solution(7796575029792550873)
XLA Ops:
  0.6 0.9 fusion.29
  1.5 0.7 convert_add_fusion
  2.2 2.4 fusion.46
  4.6 71.6 %shard_map.154 = (bf16[4,128,1024]{2,1,0:T(8,128)(2,1)}, bf16[4,128,1024]{2,1,0:T(8,128)(2,1)}, bf16[4,4,64,2048]{3,2,1,0:T(8,128)(2,1)}, bf16[4,4,64,2048]{3,2,1,0:T(8,128)(2,1)}) custom-call(bf16[128,1024]{1,0:T(8,128)(2,1)} %keys.1, bf16[128,1024]{1,0:T(8,128)(2,1)} %values.1, bf16[4,64,2048]{2,1,0:T(8,128)(2,1)} %bitcast.137, bf16[4,64,2048]{2,1,0:T(8,128)(2,1)} %bitcast.131), custom_call_target="tpu_custom_call" | custom-call | tf_op jit(solution)/shard_map/pallas_call | solution.py:394
  76.2 1.5 copy.68
  77.7 0.7 copy.44
  78.4 0.5 fusion.42
  78.9 1.3 copy-done.2
  80.3 1.9 fusion.65
  82.2 0.3 copy.67
  82.5 3.8 %convolution_convert_fusion.1 = bf16[8,128,128]{2,1,0:T(8,128)(2,1)S(1)} fusion(bf16[512,8,128]{2,1,0:T(8,128)(2,1)S(1)} %bitcast.138, f32[8,128]{1,0:T(8,128)S(1)} %get-tuple-element.32, f32[8,512,128]{2,1,0:T(8,128)} %copy-done.2), kind=kOutput, calls=%fused_computation.40 | convolution fusion | flops 136971776 | bytes 3411968 | tf_op jit(solution)/shard_map/hts,shd->thd/dot_general | solution.py:477
  86.3 3.1 multiply_reduce_fusion.2
  89.4 1.6 fusion.36
  91.0 49.4 %shard_map.155 = bf16[4,4,64,2048]{3,2,1,0:T(8,128)(2,1)} custom-call(bf16[4,64,2048]{2,1,0:T(8,128)(2,1)} %bitcast.130), custom_call_target="tpu_custom_call" | custom-call | tf_op jit(solution)/shard_map/pallas_call | solution.py:394
  140.4 7.7 %fusion.11 = f32[1024,1024]{1,0:T(8,128)S(1)} fusion(bf16[1024,2048]{1,0:T(8,128)(2,1)} %bitcast.124, bf16[1,2048,1024]{2,1,0:T(8,128)(2,1)} %param.17), kind=kOutput, calls=%fused_computation.12 | convolution fusion | flops 4294967296 | bytes 12582912 | tf_op jit(solution)/shard_map/dot_general | solution.py:502
  148.1 4.5 %fusion.1 = f32[1024,1024]{1,0:T(8,128)S(1)} fusion(bf16[1024,2048]{1,0:T(8,128)(2,1)S(1)} %bitcast.144, bf16[1,1024,2048]{2,1,0:T(8,128)(2,1)S(1)} %copy-done.14), kind=kOutput, calls=%fused_computation.2 | convolution fusion | flops 4294967296 | bytes 12582912 | tf_op jit(solution)/shard_map/dot_general | solution.py:22
  152.7 6.9 %fusion.5 = f32[1024,2048]{1,0:T(8,128)} fusion(bf16[1,2048,1024]{2,1,0:T(8,128)(2,1)S(1)} %copy-done.12, f32[1024,1024]{1,0:T(8,128)S(1)} %fusion.1, f32[1024,1024]{1,0:T(8,128)S(1)} %fusion.11), kind=kOutput, calls=%fused_computation.6 | convolution fusion | flops 4301258752 | bytes 20971520 | tf_op jit(solution)/shard_map/dot_general | solution.py:22
  159.6 6.0 %fusion.7 = f32[1024,1024]{1,0:T(8,128)} fusion(bf16[1024,2048]{1,0:T(8,128)(2,1)S(1)} %bitcast.125, bf16[1,2048,1024]{2,1,0:T(8,128)(2,1)S(1)} %copy-done.12), kind=kOutput, calls=%fused_computation.8 | convolution fusion | flops 4294967296 | bytes 12582912 | tf_op jit(solution)/shard_map/dot_general | solution.py:503
  165.7 14.3 %add_convert_fusion = bf16[1024,2048]{1,0:T(8,128)(2,1)} fusion(f32[1024,2048]{1,0:T(8,128)} %fusion.5, bf16[1,2048,1024]{2,1,0:T(8,128)(2,1)S(1)} %copy-done.13, f32[1024,1024]{1,0:T(8,128)} %copy-done.16, f32[1024,1024]{1,0:T(8,128)} %copy-done.17, f32[1024,1024]{1,0:T(8,128)} %fusion.7), kind=kOutput, calls=%fused_computation.1 | convolution fusion | flops 4309647360 | bytes 29360128 | tf_op jit(solution)/shard_map/dot_general | solution.py:22
  180.0 40.0 %shard_map.157 = bf16[4,64,2048]{2,1,0:T(8,128)(2,1)} custom-call(bf16[4,4,64,2048]{3,2,1,0:T(8,128)(2,1)} %bitcast.126), custom_call_target="tpu_custom_call" | custom-call | tf_op jit(solution)/shard_map/pallas_call | solution.py:394
  220.0 1.7 multiply_reduce_fusion.1
  221.7 0.3 add_convert_fusion.1
  222.0 0.3 copy.63
  222.3 4.2 %convert_bitcast_fusion = bf16[8,1024,256]{1,2,0:T(8,128)(2,1)} fusion(bf16[128,8,256]{0,2,1:T(8,128)(2,1)S(1)} %bitcast.133, bf16[128,1024,1]{0,1,2:T(8,128)(2,1)} %bitcast.135), kind=kOutput, calls=%fused_computation.14 | convolution fusion | flops 538968064 | bytes 4980736 | tf_op jit(solution)/shard_map/ta,tpc->pac/dot_general | solution.py:544
  226.5 6.5 %copy.53 = bf16[8,1024,256]{2,1,0:T(8,128)(2,1)} copy(bf16[8,1024,256]{1,2,0:T(8,128)(2,1)} %convert_bitcast_fusion) | data formatting | bytes 8388608 | tf_op jit(solution)/shard_map/convert_element_type | solution.py:549
  232.9 3.7 convolution_convert_fusion.2
  236.6 0.2 copy.65
  236.8 0.7 copy-done.10
  237.5 4.2 %fusion.26 = bf16[512,8,128]{0,2,1:T(8,128)(2,1)} fusion(bf16[128,8,128]{0,2,1:T(8,128)(2,1)S(1)} %bitcast.142, f32[8,128]{1,0:T(8,128)S(1)} %get-tuple-element.32, f32[8,512,128]{2,1,0:T(8,128)} %copy-done.2), kind=kOutput, calls=%fused_computation.37 | convolution fusion | flops 137364992 | bytes 3411968 | tf_op jit(solution)/shard_map/hts,thd->shd/dot_general | solution.py:569
  241.7 1.3 reshape.111
  243.0 1.5 copy.62
  244.5 2.6 multiply_reduce_fusion
  247.1 0.0 copy-done.1
  247.2 0.3 multiply_convert_fusion.7
  247.4 0.4 fusion.27
  247.9 1.6 copy.47
  249.5 2.3 stack_reshape.8
  251.8 3.1 pad_maximum_fusion.parts
  254.9 52.5 %shard_map.158 = (bf16[2,128,1024]{2,1,0:T(8,128)(2,1)}, bf16[8,256,256]{2,1,0:T(8,128)(2,1)}) custom-call(bf16[4,2,128,1024]{3,2,1,0:T(8,128)(2,1)} %pad_maximum_fusion.parts, bf16[8,4,256,256]{3,2,1,0:T(8,128)(2,1)} %bitcast.122), custom_call_target="tpu_custom_call" | custom-call | tf_op jit(solution)/shard_map/pallas_call | solution.py:394
  307.4 2.7 convert_bitcast_fusion.1
  310.1 2.9 copy.54
  313.1 2.9 copy.56
  315.9 1.9 slice_bitcast_fusion
  317.8 1.1 fusion.28
  318.9 1.8 copy.55
  320.7 11.1 %fusion.14 = bf16[1024,2048]{1,0:T(8,128)(2,1)} fusion(bf16[1,1024,2048]{2,1,0:T(8,128)(2,1)} %param.19, f32[1024,1024]{1,0:T(8,128)} %fusion.7, f32[1024,1024]{1,0:T(8,128)} %copy-done.16), kind=kOutput, calls=%fused_computation.20 | convolution fusion | flops 4303355904 | bytes 16777216 | tf_op jit(solution)/shard_map/dot_general | solution.py:505
  331.9 41.4 %shard_map.156 = bf16[4,64,2048]{2,1,0:T(8,128)(2,1)} custom-call(bf16[4,4,64,2048]{3,2,1,0:T(8,128)(2,1)} %bitcast.127), custom_call_target="tpu_custom_call" | custom-call | tf_op jit(solution)/shard_map/pallas_call | solution.py:394
  373.3 2.4 fusion.19
  (35 shorter events, 0.1 us)
Async XLA Ops:
  0.6 77.8 %copy-start = (bf16[128,1024]{1,0:T(8,128)(2,1)S(1)}, bf16[128,1024]{1,0:T(8,128)(2,1)}, u32[]{:S(2)}) copy-start(bf16[128,1024]{1,0:T(8,128)(2,1)} %param.12) | copy-start | bytes 786436
  78.4 3.8 %copy-start.8 = (bf16[4,128,1024]{2,1,0:T(8,128)(2,1)S(1)}, bf16[4,128,1024]{2,1,0:T(8,128)(2,1)}, u32[]{:S(2)}) copy-start(bf16[4,128,1024]{2,1,0:T(8,128)(2,1)} %get-tuple-element.12) | copy-start | bytes 3145732
  78.9 1.3 copy-start.2
  82.4 3.8 %copy-start.7 = (bf16[64,8,8,128]{3,2,1,0:T(8,128)(2,1)}, bf16[64,8,8,128]{3,2,1,0:T(8,128)(2,1)S(1)}, u32[]{:S(2)}) copy-start(bf16[64,8,8,128]{3,2,1,0:T(8,128)(2,1)S(1)} %copy.67) | copy-start | bytes 3145732
  82.5 3.8 %copy-start.9 = (bf16[128,2048]{1,0:T(8,128)(2,1)S(1)}, bf16[128,2048]{1,0:T(8,128)(2,1)}, u32[]{:S(2)}) copy-start(bf16[128,2048]{1,0:T(8,128)(2,1)} %param.11) | copy-start | bytes 1572868
  86.2 54.1 %copy-start.6 = (bf16[8,128,128]{2,1,0:T(8,128)(2,1)}, bf16[8,128,128]{2,1,0:T(8,128)(2,1)S(1)}, u32[]{:S(2)}) copy-start(bf16[8,128,128]{2,1,0:T(8,128)(2,1)S(1)} %convolution_convert_fusion.1) | copy-start | bytes 786436
  86.3 3.1 copy-start.11
  140.4 7.7 %copy-start.14 = (bf16[1,1024,2048]{2,1,0:T(8,128)(2,1)S(1)}, bf16[1,1024,2048]{2,1,0:T(8,128)(2,1)}, u32[]{:S(2)}) copy-start(bf16[1,1024,2048]{2,1,0:T(8,128)(2,1)} %param.19) | copy-start | bytes 12582916
  140.4 7.7 %copy-start.15 = (bf16[4,4,64,2048]{3,2,1,0:T(8,128)(2,1)S(1)}, bf16[4,4,64,2048]{3,2,1,0:T(8,128)(2,1)}, u32[]{:S(2)}) copy-start(bf16[4,4,64,2048]{3,2,1,0:T(8,128)(2,1)} %get-tuple-element.15) | copy-start | bytes 12582916
  148.1 4.6 %copy-start.16 = (f32[1024,1024]{1,0:T(8,128)}, f32[1024,1024]{1,0:T(8,128)S(1)}, u32[]{:S(2)}) copy-start(f32[1024,1024]{1,0:T(8,128)S(1)} %fusion.11) | copy-start | bytes 12582916
  148.1 4.6 %copy-start.12 = (bf16[1,2048,1024]{2,1,0:T(8,128)(2,1)S(1)}, bf16[1,2048,1024]{2,1,0:T(8,128)(2,1)}, u32[]{:S(2)}) copy-start(bf16[1,2048,1024]{2,1,0:T(8,128)(2,1)} %param.18) | copy-start | bytes 12582916
  152.6 7.0 %copy-start.17 = (f32[1024,1024]{1,0:T(8,128)}, f32[1024,1024]{1,0:T(8,128)S(1)}, u32[]{:S(2)}) copy-start(f32[1024,1024]{1,0:T(8,128)S(1)} %fusion.1) | copy-start | bytes 12582916
  152.7 7.0 %copy-start.4 = (bf16[4,4,64,2048]{3,2,1,0:T(8,128)(2,1)S(1)}, bf16[4,4,64,2048]{3,2,1,0:T(8,128)(2,1)}, u32[]{:S(2)}) copy-start(bf16[4,4,64,2048]{3,2,1,0:T(8,128)(2,1)} %shard_map.155) | copy-start | bytes 12582916
  159.6 6.0 %copy-start.13 = (bf16[1,2048,1024]{2,1,0:T(8,128)(2,1)S(1)}, bf16[1,2048,1024]{2,1,0:T(8,128)(2,1)}, u32[]{:S(2)}) copy-start(bf16[1,2048,1024]{2,1,0:T(8,128)(2,1)} %param.17) | copy-start | bytes 12582916
  180.0 41.7 %copy-start.5 = (bf16[128,2048]{1,0:T(8,128)(2,1)S(1)}, bf16[128,2048]{1,0:T(8,128)(2,1)}, u32[]{:S(2)}) copy-start(bf16[128,2048]{1,0:T(8,128)(2,1)} %param.21) | copy-start | bytes 1572868
  222.0 10.9 %copy-start.3 = (bf16[128,2048]{1,0:T(8,128)(2,1)}, bf16[128,2048]{1,0:T(8,128)(2,1)S(1)}, u32[]{:S(2)}) copy-start(bf16[128,2048]{1,0:T(8,128)(2,1)S(1)} %add_convert_fusion.1) | copy-start | bytes 1572868
  236.8 0.7 copy-start.10
  244.5 2.6 copy-start.1

commit v2 on v1

--- a/solution.py
+++ b/solution.py
@@ -37,8 +37,7 @@
 def flip(index, mask, size):
     total, bit = 0, 1
     while bit < size:
-        here = lax.rem(lax.div(index, bit), 2)
-        total = total + bit * ((1 - here) if (mask // bit) % 2 else here)
+        total = total + bit * lax.rem(lax.div(index, bit) + (mask // bit), 2)
         bit *= 2
     return total
 
@@ -173,19 +172,6 @@
     for copy in passed:
         copy.wait_recv()
     wire.finish()
-
-
-def dispatch_kernel(sizes, rows, out, send_sems, recv_sems, own_sem):
-    wire = Wire(sizes, send_sems, recv_sems)
-    own = pltpu.make_async_copy(
-        rows.at[wire.expert], out.at[wire.dp, wire.expert], own_sem
-    )
-    own.start()
-    wire.greet()
-    crossing = cross(wire, rows, out)
-    passed = spread(wire, rows, out, crossing)
-    settle(wire, passed)
-    own.wait()
 
 
 def opening_kernel(
@@ -266,26 +252,6 @@
     return added(
         near_in[wire.high, index], *[far_in[m - 1, index] for m in range(1, wire.outer)]
     )
-
-
-def return_kernel(sizes, parts, out, near_in, far_in, total, send_sems, recv_sems):
-    wire = Wire(sizes, send_sems, recv_sems)
-    wire.greet()
-    masks = wire.expert_masks() + [0]
-    chunks = [(m, wire.expert_at(m)) for m in masks]
-    flows = fold_start(wire, parts, near_in, chunks)
-    far = {c: fold_near(wire, flows, parts, near_in, far_in, c, index) for c, index in chunks}
-    arriving = []
-    for c, index in chunks:
-        summed = fold_far(wire, far[c], near_in, far_in, index)
-        if c == 0:
-            out[index] = summed
-        else:
-            total[index] = summed
-            arriving.append(
-                wire.send(total.at[index], out.at[wire.expert], wire.to_expert(c))
-            )
-    settle(wire, arriving)
 
 
 def closing_kernel(
@@ -405,6 +371,263 @@
     )(*operands)
 
 
+def expert_kernel(
+    sizes, rows, grads, gate_hbm, up_hbm, down_hbm, grad_back, back,
+    gathered, gate, up, down, act, gate_grad, up_grad, parts, near_in, far_in, total,
+    zs, zr, hs, hr, ls, lr, fls, flr, fhs, fhr, fzs, fzr, weight_sems, own_sem,
+):
+    wire = Wire(sizes, None, None)
+    experts, outer, ways = wire.experts, wire.outer, wire.ways
+    capacity, width = rows.shape[1], rows.shape[2]
+    hidden_units = gate.shape[1]
+    backs = (grad_back, back)
+    loads = [
+        pltpu.make_async_copy(source.at[0], target, weight_sems.at[i])
+        for i, (source, target) in enumerate(((gate_hbm, gate), (up_hbm, up), (down_hbm, down)))
+    ]
+    own = pltpu.make_async_copy(
+        rows.at[wire.expert], gathered.at[wire.dp, wire.expert], own_sem
+    )
+    own.start()
+    for load in loads:
+        load.start()
+    wire.greet()
+
+    def link(source, target, send_sem, recv_sem, peer):
+        return pltpu.make_async_remote_copy(
+            src_ref=source, dst_ref=target, send_sem=send_sem, recv_sem=recv_sem,
+            device_id=peer, device_id_type=MESH,
+        )
+
+    def over_expert(mask):
+        return link(
+            rows.at[wire.expert_at(mask)], gathered.at[wire.dp, wire.expert],
+            zs.at[mask], zr.at[mask], wire.to_expert(mask),
+        )
+
+    def over_high(m, mask):
+        block = gathered.at[wire.dp, wire.expert_at(mask)]
+        return link(block, block, hs.at[m - 1, mask], hr.at[m - 1, mask], wire.to_high(m))
+
+    def over_low(m, mask):
+        block = gathered.at[wire.dp_at(m) if m else wire.dp, wire.expert_at(mask)]
+        return link(block, block, ls.at[m, mask], lr.at[m, mask], wire.to_low())
+
+    def back_low(r, h, mask):
+        index = wire.expert_at(mask)
+        return link(
+            parts.at[r, h * 2 + (1 - wire.low), index], near_in.at[r, h, index],
+            fls.at[r, h, mask], flr.at[r, h, mask], wire.to_low(),
+        )
+
+    def back_high(r, m, mask):
+        index = wire.expert_at(mask)
+        return link(
+            near_in.at[r, wire.high_at(m), index], far_in.at[r, m - 1, index],
+            fhs.at[r, m - 1, mask], fhr.at[r, m - 1, mask], wire.to_high(m),
+        )
+
+    def back_expert(r, mask):
+        index = wire.expert_at(mask)
+        return link(
+            total.at[r, index], backs[r].at[wire.expert],
+            fzs.at[r, mask], fzr.at[r, mask], wire.to_expert(mask),
+        )
+
+    def fold_low(r, mask):
+        index = wire.expert_at(mask)
+        for h in range(outer):
+            back_low(r, h, mask).wait_recv()
+            near_in[r, h, index] = added(parts[r, h * 2 + wire.low, index], near_in[r, h, index])
+        for m in range(1, outer):
+            back_high(r, m, mask).start()
+
+    def fold_high(r, mask, position):
+        index = wire.expert_at(mask)
+        for m in range(1, outer):
+            back_high(r, m, mask).wait_recv()
+        summed = added(
+            near_in[r, wire.high, index], *[far_in[r, m - 1, index] for m in range(1, outer)]
+        )
+
+        @pl.when(position == 0)
+        def _():
+            backs[r][index] = summed
+
+        @pl.when(position > 0)
+        def _():
+            total[r, index] = summed
+            back_expert(r, mask).start()
+
+    tile = 256
+
+    def units(mask):
+        index = wire.expert_at(mask)
+
+        @pl.loop(0, hidden_units // tile)
+        def _(j):
+            columns = pl.ds(pl.multiple_of(j * tile, tile), tile)
+            block = gathered[:, index].reshape(ways * capacity, width)
+            grad_block = grads[:, index].reshape(ways * capacity, width)
+            gate_pre = jnp.dot(block, gate[:, columns], preferred_element_type=jnp.float32)
+            up_pre = jnp.dot(block, up[:, columns], preferred_element_type=jnp.float32)
+            grad_act = contract_last(grad_block, down[columns, :])
+            sigmoid_gate = jax.nn.sigmoid(gate_pre)
+            silu = gate_pre * sigmoid_gate
+            act[:, columns] = (silu * up_pre).astype(jnp.bfloat16)
+            gate_grad[:, columns] = (
+                grad_act * up_pre * sigmoid_gate * (1.0 + gate_pre * (1.0 - sigmoid_gate))
+            ).astype(jnp.bfloat16)
+            up_grad[:, columns] = (grad_act * silu).astype(jnp.bfloat16)
+
+    def grad_products(mask):
+        index = wire.expert_at(mask)
+
+        @pl.loop(0, width // tile)
+        def _(j):
+            columns = pl.ds(pl.multiple_of(j * tile, tile), tile)
+            piece = contract_last(gate_grad[...], gate[columns, :]) + contract_last(
+                up_grad[...], up[columns, :]
+            )
+            parts[0, :, index, :, columns] = piece.astype(jnp.bfloat16).reshape(
+                ways, capacity, tile
+            )
+
+    def out_products(mask):
+        index = wire.expert_at(mask)
+
+        @pl.loop(0, width // tile)
+        def _(j):
+            columns = pl.ds(pl.multiple_of(j * tile, tile), tile)
+            piece = jnp.dot(act[...], down[:, columns], preferred_element_type=jnp.float32)
+            parts[1, :, index, :, columns] = piece.astype(jnp.bfloat16).reshape(
+                ways, capacity, tile
+            )
+
+    for step in range(1, experts):
+        over_expert(experts - step).start()
+    own.wait()
+
+    def mask_of(position):
+        return lax.rem(experts - position, experts)
+
+    @pl.loop(0, experts + 2)
+    def _(step):
+        incoming, current, leaving = step < experts, step >= 1, step >= 2
+        now, before, last = mask_of(step), mask_of(step - 1), mask_of(step - 2)
+
+        @pl.when(incoming)
+        def _():
+            @pl.when(step > 0)
+            def _():
+                over_expert(now).wait_recv()
+
+            for m in range(1, outer):
+                over_high(m, now).start()
+            over_low(0, now).start()
+
+        @pl.when(leaving)
+        def _():
+            fold_low(1, last)
+
+        @pl.when(step == 1)
+        def _():
+            for load in loads:
+                load.wait()
+
+        busy = current & (step <= experts)
+
+        @pl.when(busy)
+        def _():
+            for m in range(outer):
+                over_low(m, before).wait_recv()
+            units(before)
+            grad_products(before)
+            for h in range(outer):
+                back_low(0, h, before).start()
+
+        @pl.when(incoming)
+        def _():
+            for m in range(1, outer):
+                over_high(m, now).wait_recv()
+                over_low(m, now).start()
+
+        @pl.when(leaving)
+        def _():
+            fold_high(0, last, step - 2)
+
+        @pl.when(busy)
+        def _():
+            out_products(before)
+            fold_low(0, before)
+            for h in range(outer):
+                back_low(1, h, before).start()
+
+        @pl.when(leaving)
+        def _():
+            fold_high(1, last, step - 2)
+
+    for mask in range(experts):
+        for r in range(2):
+            if mask:
+                back_expert(r, mask).wait()
+            for h in range(outer):
+                back_low(r, h, mask).wait_send()
+            for m in range(1, outer):
+                back_high(r, m, mask).wait_send()
+        if mask:
+            over_expert(mask).wait_send()
+        for m in range(1, outer):
+            over_high(m, mask).wait_send()
+        for m in range(outer):
+            over_low(m, mask).wait_send()
+
+
+def run_experts(sizes, ident, rows, grads, gate_weight, up_weight, down_weight):
+    sections, experts, ways = sizes
+    outer = ways // 2
+    span = max(outer - 1, 1)
+    buckets = rows.shape
+    count = ways * buckets[1]
+    units = gate_weight.shape[2]
+    anywhere = pl.BlockSpec(memory_space=pl.ANY)
+    low = lambda *shape: pltpu.VMEM(shape, jnp.bfloat16)
+    sems = []
+    for shape in (
+        (experts,),
+        (span, experts),
+        (outer, experts),
+        (2, outer, experts),
+        (2, span, experts),
+        (2, experts),
+    ):
+        sems += [pltpu.SemaphoreType.DMA(shape)] * 2
+    return pl.pallas_call(
+        functools.partial(expert_kernel, sizes),
+        out_shape=[jax.ShapeDtypeStruct(buckets, jnp.bfloat16)] * 2,
+        in_specs=[WHOLE, WHOLE, anywhere, anywhere, anywhere],
+        out_specs=[WHOLE, WHOLE],
+        scratch_shapes=[
+            low(ways, *buckets),
+            low(*gate_weight.shape[1:]),
+            low(*up_weight.shape[1:]),
+            low(*down_weight.shape[1:]),
+            low(count, units),
+            low(count, units),
+            low(count, units),
+            low(2, ways, *buckets),
+            low(2, outer, *buckets),
+            low(2, span, *buckets),
+            low(2, *buckets),
+        ]
+        + sems
+        + [pltpu.SemaphoreType.DMA((3,)), pltpu.SemaphoreType.DMA],
+        compiler_params=pltpu.CompilerParams(
+            collective_id=ident, has_side_effects=True, vmem_limit_bytes=62 * 1024 * 1024
+        ),
+    )(rows, grads, gate_weight, up_weight, down_weight)
+
+
 def shards(
     residual,
     queries,
@@ -485,54 +708,11 @@
     unit_rows = hidden * inv_rms
     normed = (unit_rows * norm_gain).astype(jnp.bfloat16)
     send_buffer = jnp.dot(placing, normed).reshape(buckets)
-    gate_local = gate_weight[0]
-    up_local = up_weight[0]
-    down_local = down_weight[0]
-    block_width = FF // data_ways
-    (gathered,) = call(
-        dispatch_kernel,
-        sizes,
-        1,
-        experts * (1 + 2 * outer),
-        (send_buffer,),
-        (spread_shape,),
-        extra=(pltpu.SemaphoreType.DMA,),
-    )
-    flattened = gathered.reshape(-1, D)
-    gate_pre = jnp.dot(flattened, gate_local, preferred_element_type=jnp.float32)
-    up_pre = jnp.dot(flattened, up_local, preferred_element_type=jnp.float32)
-    activated = (jax.nn.silu(gate_pre) * up_pre).astype(jnp.bfloat16)
-    partial_out = jnp.dot(activated, down_local, preferred_element_type=jnp.float32)
-    back_copies = experts * (1 + outer + outer)
-    back_scratch = ((outer,) + buckets, (max(outer - 1, 1),) + buckets, buckets)
-    (returned,) = call(
-        return_kernel,
-        sizes,
-        2,
-        back_copies,
-        (partial_out.astype(jnp.bfloat16).reshape(spread_shape),),
-        (buckets,),
-        back_scratch,
+    grad_returned, returned = run_experts(
+        sizes, 1, send_buffer, grad_gathered, gate_weight, up_weight, down_weight
     )
     expert_back = contract_first(placing, returned.reshape(experts * capacity, D))
     layer_out = (hidden + expert_back.astype(jnp.float32)).astype(jnp.bfloat16)
-    grad_flat = grad_gathered.reshape(-1, D)
-    sigmoid_gate = jax.nn.sigmoid(gate_pre)
-    grad_act = contract_last(grad_flat, down_local)
-    grad_gate = (grad_act * up_pre * sigmoid_gate * (1.0 + gate_pre * (1.0 - sigmoid_gate))).astype(
-        jnp.bfloat16
-    )
-    grad_up = (grad_act * jax.nn.silu(gate_pre)).astype(jnp.bfloat16)
-    partial_grad = contract_last(grad_gate, gate_local) + contract_last(grad_up, up_local)
-    (grad_returned,) = call(
-        return_kernel,
-        sizes,
-        3,
-        back_copies,
-        (partial_grad.astype(jnp.bfloat16).reshape(spread_shape),),
-        (buckets,),
-        back_scratch,
-    )
     grad_normed = contract_first(placing, grad_returned.reshape(experts * capacity, D))
     scaled = grad_normed * norm_gain
     resid_grad = (
@@ -581,7 +761,7 @@
     key_value, weight_parts = call(
         closing_kernel,
         sizes,
-        4,
+        2,
         4 * outer + experts * (1 + sections + outer + 1) + 3 * ways,
         (pair_parts, products.reshape(ways, experts, weight_rows, width)),
         (pair, (ways,) + block),

time: 377 us -> 303 us (0.80)
  matrix products: 83.1 us -> 25 us
  Pallas kernels: 255 us -> 244 us
    pallas_call x5 -> x2, Pallas kernels: 255 us -> 124 us  [call(): pl.pallas_call(functools.partial(kernel, sizes), out_shape=[low(s) for s...]
    pallas_call x0 -> x1, Pallas kernels: none -> 120 us  [run_experts(): pl.pallas_call(functools.partial(expert_kernel, sizes), out_shape=[jax.Sh...]
    dot_general x4 -> x1, matrix products: 29.5 us -> 1.51 us  [contract_last(): lax.dot_general(left_side, right_side, (((1,), (1,)), ((), ())), preferre...]
    dot_general x3 -> x0, matrix products: 24.8 us -> none  [the longest x1 11.1 us: shards(): jnp.dot(activated, down_local, preferred_element_type=jnp.float32)]
    unnamed x40 -> x36, local copies, waits for them, and re-layouts: 8.57 us -> 9.14 us
where the time goes in v2:
time: 303 us; the launch traced here: 302 us
  Pallas kernels  244 us (81%)
  local copies, waits for them, and re-layouts  26.1 us (9%)
  matrix products  25 us (8%)
  other arithmetic  6.23 us (2%)
    pallas_call x2, Pallas kernels, call(): pl.pallas_call(functools.partial(kernel, sizes), out_shape=[low(s) for s...  124 us
    pallas_call x1, Pallas kernels, run_experts(): pl.pallas_call(functools.partial(expert_kernel, sizes), out_shape=[jax.Sh...  120 us
    unnamed x36, local copies, waits for them, and re-layouts  9.14 us
    convert_element_type x1, local copies, waits for them, and re-layouts, shards(): products = jnp.einsum('ta,tpc->pac', attended, resid_grad.reshape(tokens_...  6.47 us

profile of v2, /device:TPU:0, one launch (start us, length us, event | category | flops | bytes accessed | tf_op | source)
XLA Modules:
  0.0 301.8 jit_solution(14819072560853287974)
XLA Ops:
  0.6 0.0 copy-start
  0.6 0.9 fusion.10
  1.5 0.7 convert_add_fusion
  2.2 2.4 fusion.25
  4.6 71.6 %shard_map.154 = (bf16[4,128,1024]{2,1,0:T(8,128)(2,1)}, bf16[4,128,1024]{2,1,0:T(8,128)(2,1)}, bf16[4,4,64,2048]{3,2,1,0:T(8,128)(2,1)}, bf16[4,4,64,2048]{3,2,1,0:T(8,128)(2,1)}) custom-call(bf16[128,1024]{1,0:T(8,128)(2,1)} %keys.1, bf16[128,1024]{1,0:T(8,128)(2,1)} %values.1, bf16[4,64,2048]{2,1,0:T(8,128)(2,1)} %bitcast.105, bf16[4,64,2048]{2,1,0:T(8,128)(2,1)} %bitcast.99), custom_call_target="tpu_custom_call" | custom-call | tf_op jit(solution)/shard_map/pallas_call | solution.py:360
  76.2 2.6 copy.67
  78.8 0.3 copy.68
  79.1 0.7 copy.44
  79.8 0.0 copy-done
  79.8 0.0 copy-start.2
  79.8 0.5 fusion.21
  80.3 2.0 fusion.41
  82.3 0.0 copy-done.5
  82.3 2.3 convolution_convert_fusion.1
  84.7 0.0 copy-start.10
  84.7 0.0 copy-start.15
  84.7 3.2 %multiply_reduce_fusion.2 = (f32[128]{0:T(128)S(1)}, f32[128,2048]{1,0:T(8,128)S(1)}) fusion(bf16[128,1024]{0,1:T(8,128)(2,1)S(1)} %bitcast.102, bf16[1024,2048]{1,0:T(8,128)(2,1)} %bitcast.94, bf16[128,2048]{1,0:T(8,128)(2,1)} %param.11), kind=kOutput, calls=%fused_computation.28 | convolution fusion | flops 537919360 | bytes 6029824 | tf_op jit(solution)/shard_map/dot_general | solution.py:704
  87.9 1.5 fusion.15
  89.5 119.6 %shard_map.155 = (bf16[4,64,2048]{2,1,0:T(8,128)(2,1)}, bf16[4,64,2048]{2,1,0:T(8,128)(2,1)}) custom-call(bf16[4,64,2048]{2,1,0:T(8,128)(2,1)} %bitcast.98, bf16[4,4,64,2048]{3,2,1,0:T(8,128)(2,1)} %get-tuple-element.17.grads, bf16[1,2048,1024]{2,1,0:T(8,128)(2,1)} %gate_hbm.1, bf16[1,2048,1024]{2,1,0:T(8,128)(2,1)} %up_hbm.1, bf16[1,1024,2048]{2,1,0:T(8,128)(2,1)} %down_hbm.1), custom_call_target="tpu_custom_call" | custom-call | tf_op jit(solution)/shard_map/pallas_call | solution.py:605
  209.1 2.5 fusion.1
  211.5 0.4 multiply_reduce_fusion.1
  212.0 0.6 copy-done.9
  212.6 0.3 add_convert_fusion
  212.9 1.0 copy-done.1
  213.9 1.5 convolution_convert_fusion.2
  215.4 0.2 copy.65
  215.6 3.3 %fusion.7 = bf16[512,8,128]{0,2,1:T(8,128)(2,1)S(1)} fusion(bf16[128,8,128]{0,2,1:T(8,128)(2,1)S(1)} %bitcast.112, f32[8,128]{1,0:T(8,128)S(1)} %get-tuple-element.36, f32[8,512,128]{2,1,0:T(8,128)} %copy-done.5), kind=kOutput, calls=%fused_computation.17 | convolution fusion | flops 137364992 | bytes 3411968 | tf_op jit(solution)/shard_map/hts,thd->shd/dot_general | solution.py:749
  218.8 1.2 reshape.95
  220.0 2.6 copy.62
  222.6 1.0 copy.63
  223.6 1.7 multiply_reduce_fusion
  225.3 0.3 multiply_convert_fusion.1
  225.6 0.9 copy-done.3
  226.5 1.1 fusion.9
  227.7 0.4 fusion.8
  228.1 0.7 copy.47
  228.8 0.5 stack_reshape.8
  229.3 0.0 copy-done.7
  229.3 0.0 copy-start.11
  229.3 1.5 pad_maximum_fusion.parts
  230.8 0.8 copy.55
  231.7 3.2 %convert_bitcast_fusion = bf16[8,1024,256]{1,2,0:T(8,128)(2,1)} fusion(bf16[128,8,256]{0,2,1:T(8,128)(2,1)S(1)} %bitcast.101, bf16[128,1024,1]{0,1,2:T(8,128)(2,1)S(1)} %bitcast.103), kind=kOutput, calls=%fused_computation.1 | convolution fusion | flops 538968064 | bytes 4980736 | tf_op jit(solution)/shard_map/ta,tpc->pac/dot_general | solution.py:724
  234.9 6.5 %copy.53 = bf16[8,1024,256]{2,1,0:T(8,128)(2,1)} copy(bf16[8,1024,256]{1,2,0:T(8,128)(2,1)} %convert_bitcast_fusion) | data formatting | bytes 8388608 | tf_op jit(solution)/shard_map/convert_element_type | solution.py:729
  241.4 52.4 %shard_map.156 = (bf16[2,128,1024]{2,1,0:T(8,128)(2,1)}, bf16[8,256,256]{2,1,0:T(8,128)(2,1)}) custom-call(bf16[4,2,128,1024]{3,2,1,0:T(8,128)(2,1)} %pad_maximum_fusion.parts, bf16[8,4,256,256]{3,2,1,0:T(8,128)(2,1)} %bitcast.96), custom_call_target="tpu_custom_call" | custom-call | tf_op jit(solution)/shard_map/pallas_call | solution.py:360
  293.8 1.9 slice_bitcast_fusion
  295.6 1.4 convert_bitcast_fusion.1
  297.1 1.9 copy.54
  298.9 2.9 copy.56
  (23 shorter events, 0.1 us)
Async XLA Ops:
  0.6 79.1 %copy-start = (bf16[128,1024]{1,0:T(8,128)(2,1)S(1)}, bf16[128,1024]{1,0:T(8,128)(2,1)}, u32[]{:S(2)}) copy-start(bf16[128,1024]{1,0:T(8,128)(2,1)} %param.12) | copy-start | bytes 786436
  76.2 2.6 copy-start.14
  79.8 2.5 copy-start.2
  80.3 2.0 copy-start.5
  84.7 3.2 %copy-start.10 = (bf16[8,128,128]{2,1,0:T(8,128)(2,1)}, bf16[8,128,128]{2,1,0:T(8,128)(2,1)S(1)}, u32[]{:S(2)}) copy-start(bf16[8,128,128]{2,1,0:T(8,128)(2,1)S(1)} %convolution_convert_fusion.1) | copy-start | bytes 786436
  84.7 3.3 %copy-start.15 = (f32[2048]{0:T(1024)S(1)}, f32[2048]{0:T(1024)}, u32[]{:S(2)}) copy-start(f32[2048]{0:T(1024)} %param.16) | copy-start | bytes 24580
  209.0 2.5 copy-start.13
  211.5 1.0 copy-start.9
  211.5 2.4 copy-start.1
  213.9 8.7 %copy-start.6 = (bf16[128,2048]{1,0:T(8,128)(2,1)}, bf16[128,2048]{1,0:T(8,128)(2,1)S(1)}, u32[]{:S(2)}) copy-start(bf16[128,2048]{1,0:T(8,128)(2,1)S(1)} %add_convert_fusion) | copy-start | bytes 1572868
  220.0 3.6 %copy-start.4 = (f32[8,128,512]{1,2,0:T(8,128)S(1)}, f32[8,128,512]{1,2,0:T(8,128)}, u32[]{:S(2)}) copy-start(f32[8,128,512]{1,2,0:T(8,128)} %get-tuple-element.37) | copy-start | bytes 6291460
  225.3 1.2 copy-start.3
  228.1 1.2 copy-start.7
  229.3 1.5 copy-start.12
  229.3 2.4 copy-start.8
  229.3 2.4 copy-start.11

commit v3 on v2

--- a/solution.py
+++ b/solution.py
@@ -142,9 +142,15 @@
     }
 
 
-def spread(wire, source, out, crossing):
-    passed = []
-    held = None
+def spread_own(wire, source, out):
+    block, target = source.at[wire.expert], out.at[wire.dp, wire.expert]
+    wide = [wire.send(block, target, wire.to_high(m)) for m in range(1, wire.outer)]
+    return wide, wire.send(block, target, wire.to_low())
+
+
+def spread(wire, out, crossing, first):
+    passed = [first[1]]
+    held = (0, first[0])
 
     def hand_over(mask, wide):
         for m, copy in enumerate(wide, 1):
@@ -152,17 +158,12 @@
             block = out.at[wire.dp_at(m), wire.expert_at(mask)]
             passed.append(wire.send(block, block, wire.to_low()))
 
-    for mask in [0] + wire.expert_masks():
-        target = out.at[wire.dp, wire.expert_at(mask)]
-        if mask:
-            crossing[mask].wait_recv()
-            block = target
-        else:
-            block = source.at[wire.expert]
-        wide = [wire.send(block, target, wire.to_high(m)) for m in range(1, wire.outer)]
-        passed.append(wire.send(block, target, wire.to_low()))
-        if held is not None:
-            hand_over(*held)
+    for mask in wire.expert_masks():
+        block = out.at[wire.dp, wire.expert_at(mask)]
+        crossing[mask].wait_recv()
+        wide = [wire.send(block, block, wire.to_high(m)) for m in range(1, wire.outer)]
+        passed.append(wire.send(block, block, wire.to_low()))
+        hand_over(*held)
         held = (mask, wide)
     hand_over(*held)
     return passed
@@ -195,27 +196,39 @@
     wire.greet(sections=True)
     key_flow = gather_start(wire, keys, keys_out)
     value_flow = gather_start(wire, values, values_out)
-    part = wire.section * 2 + wire.low
-    crossing = cross(wire, rows, out)
-    quarters = {
+    outer, sections = wire.outer, wire.sections
+
+    def piece(mask, section, high):
+        return weight_out.at[wire.expert_at(mask), (section * 2 + wire.low) * outer + high]
+
+    part = (wire.section * 2 + wire.low) * outer + wire.high
+    pieces = {
         m: wire.send(weight.at[part], weight_out.at[wire.expert, part], wire.to_expert(m))
         for m in wire.expert_masks()
     }
+    crossing = cross(wire, rows, out)
     passed = gather_end(wire, key_flow, keys_out) + gather_end(wire, value_flow, values_out)
-    passed += spread(wire, rows, out, crossing)
-    sideways = {}
+    wides, sides = [], []
     for mask in wire.expert_masks():
-        quarters[mask].wait_recv()
-        block = weight_out.at[wire.expert_at(mask), part]
-        sideways[mask] = [
-            wire.send(block, block, wire.to_section(m)) for m in range(1, wire.sections)
-        ]
+        pieces[mask].wait_recv()
+        block = piece(mask, wire.section, wire.high)
+        for m in range(1, outer):
+            wides.append((mask, m, wire.send(block, block, wire.to_high(m))))
+        for s in range(1, sections):
+            sides.append((mask, 0, s, wire.send(block, block, wire.to_section(s))))
         passed.append(wire.send(block, block, wire.to_low()))
-    for mask in wire.expert_masks():
-        for m, copy in enumerate(sideways[mask], 1):
-            copy.wait_recv()
-            block = weight_out.at[wire.expert_at(mask), wire.section_at(m) * 2 + wire.low]
-            passed.append(wire.send(block, block, wire.to_low()))
+    first = spread_own(wire, rows, out)
+    for mask, m, copy in wides:
+        copy.wait_recv()
+        block = piece(mask, wire.section, wire.high_at(m))
+        for s in range(1, sections):
+            sides.append((mask, m, s, wire.send(block, block, wire.to_section(s))))
+        passed.append(wire.send(block, block, wire.to_low()))
+    passed += spread(wire, out, crossing, first)
+    for mask, m, s, copy in sides:
+        copy.wait_recv()
+        block = piece(mask, wire.section_at(s), wire.high_at(m) if m else wire.high)
+        passed.append(wire.send(block, block, wire.to_low()))
     settle(wire, passed)
     for copy in local:
         copy.wait()
@@ -255,66 +268,51 @@
 
 
 def closing_kernel(
-    sizes, parts, products, out, weight_out,
-    near_in, far_in, low_in, side_in, high_in, total, cross_in, send_sems, recv_sems,
+    sizes, parts, features, columns, out, weight_out,
+    near_in, far_in, columns_in, total, cross_in, send_sems, recv_sems, own_sem,
 ):
     wire = Wire(sizes, send_sems, recv_sems)
-    wire.greet(sections=True)
     outer, sections = wire.outer, wire.sections
     span = outer * sections
+
+    def at(flip_low, s, m):
+        low = (1 - wire.low) if flip_low else wire.low
+        section = wire.section_at(s) if s else wire.section
+        high = wire.high_at(m) if m else wire.high
+        peer = {"section": section, "dp": high * 2 + low}
+        return (low * sections + section) * outer + high, peer
+
+    mine = at(0, 0, 0)[0]
+    own = pltpu.make_async_copy(columns.at[mine], columns_in.at[mine], own_sem)
+    own.start()
+    others = [
+        (f, s, m) for m in range(outer) for s in range(sections) for f in range(2) if f + s + m
+    ][::-1]
+    barrier = pltpu.get_barrier_semaphore()
+    peers = [at(*o)[1] for o in others] + [wire.to_expert(m) for m in range(1, wire.experts)]
+    for peer in peers:
+        pl.semaphore_signal(barrier, inc=1, device_id=peer, device_id_type=MESH)
+    pl.semaphore_wait(barrier, len(peers))
     masks = wire.expert_masks() + [0]
-    shards = [(m, wire.expert_at(m)) for m in masks]
-    lows = {
-        c: wire.send(
-            products.at[pl.ds((1 - wire.low) * span, span), index],
-            low_in.at[index],
-            wire.to_low(),
-        )
-        for c, index in shards
-    }
+    exchange = []
+    for other in others:
+        index, peer = at(*other)
+        exchange.append(wire.send(columns.at[index], columns_in.at[mine], peer))
     pairs = [(i, i) for i in range(parts.shape[1])]
     flows = fold_start(wire, parts, near_in, pairs)
-    sides = {}
-    for c, index in shards:
-        lows[c].wait_recv()
-        for p in range(span):
-            low_in[index, p] = added(products[wire.low * span + p, index], low_in[index, p])
-        sides[c] = [
-            wire.send(
-                low_in.at[index, pl.ds(wire.section_at(m) * outer, outer)],
-                side_in.at[m - 1, index],
-                wire.to_section(m),
+    far = {c: fold_near(wire, flows, parts, near_in, far_in, c, index) for c, index in pairs}
+    own.wait()
+    for copy in exchange:
+        copy.wait_recv()
+    crossing = {}
+    for c in masks:
+        index = wire.expert_at(c)
+        product = jnp.dot(features[0, index], columns_in[0], preferred_element_type=jnp.float32)
+        for p in range(1, 2 * span):
+            product = product + jnp.dot(
+                features[p, index], columns_in[p], preferred_element_type=jnp.float32
             )
-            for m in range(1, sections)
-        ]
-    far = {c: fold_near(wire, flows, parts, near_in, far_in, c, index) for c, index in pairs}
-    highs = {}
-    for c, index in shards:
-        for copy in sides[c]:
-            copy.wait_recv()
-        for h in range(outer):
-            place = wire.section * outer + h
-            low_in[index, place] = added(
-                low_in[index, place], *[side_in[m - 1, index, h] for m in range(1, sections)]
-            )
-        highs[c] = [
-            wire.send(
-                low_in.at[index, wire.section * outer + wire.high_at(m)],
-                high_in.at[m - 1, index],
-                wire.to_high(m),
-            )
-            for m in range(1, outer)
-        ]
-    crossing = {}
-    mine = None
-    for c, index in shards:
-        for copy in highs[c]:
-            copy.wait_recv()
-        summed = added(
-            low_in[index, wire.section * outer + wire.high],
-            *[high_in[m - 1, index] for m in range(1, outer)],
-        )
-        total[index] = summed
+        total[index] = product.astype(jnp.bfloat16)
         if c:
             crossing[c] = wire.send(total.at[index], cross_in.at[c - 1], wire.to_expert(c))
     for c, index in pairs:
@@ -372,9 +370,9 @@
 
 
 def expert_kernel(
-    sizes, rows, grads, gate_hbm, up_hbm, down_hbm, grad_back, back,
+    sizes, rows, grads, features, gate_hbm, up_hbm, down_hbm, grad_back, back, features_out,
     gathered, gate, up, down, act, gate_grad, up_grad, parts, near_in, far_in, total,
-    zs, zr, hs, hr, ls, lr, fls, flr, fhs, fhr, fzs, fzr, weight_sems, own_sem,
+    zs, zr, hs, hr, ls, lr, fls, flr, fhs, fhr, fzs, fzr, ps, pr, weight_sems, own_sems,
 ):
     wire = Wire(sizes, None, None)
     experts, outer, ways = wire.experts, wire.outer, wire.ways
@@ -386,12 +384,26 @@
         for i, (source, target) in enumerate(((gate_hbm, gate), (up_hbm, up), (down_hbm, down)))
     ]
     own = pltpu.make_async_copy(
-        rows.at[wire.expert], gathered.at[wire.dp, wire.expert], own_sem
+        rows.at[wire.expert], gathered.at[wire.dp, wire.expert], own_sems.at[0]
     )
     own.start()
+    sections = wire.sections
+    span = outer * sections
+
+    def place(low, section, high):
+        return (low * sections + section) * outer + high
+
+    def at_masks(s, m):
+        return (wire.section_at(s) if s else wire.section), (
+            wire.high_at(m) if m else wire.high
+        )
+
+    mine = place(wire.low, wire.section, wire.high)
+    own_features = pltpu.make_async_copy(features, features_out.at[mine], own_sems.at[1])
+    own_features.start()
     for load in loads:
         load.start()
-    wire.greet()
+    wire.greet(sections=True)
 
     def link(source, target, send_sem, recv_sem, peer):
         return pltpu.make_async_remote_copy(
@@ -432,6 +444,26 @@
         return link(
             total.at[r, index], backs[r].at[wire.expert],
             fzs.at[r, mask], fzr.at[r, mask], wire.to_expert(mask),
+        )
+
+    def plane_high(m):
+        return link(
+            features, features_out.at[mine], ps.at[0, m], pr.at[0, m], wire.to_high(m)
+        )
+
+    def plane_side(s, m):
+        block = features_out.at[place(wire.low, wire.section, at_masks(0, m)[1])]
+        return link(
+            block if m else features, block, ps.at[1, s * outer + m], pr.at[1, s * outer + m],
+            wire.to_section(s),
+        )
+
+    def plane_low(s, m):
+        section, high = at_masks(s, m)
+        block = features_out.at[place(wire.low, section, high)]
+        return link(
+            block if s + m else features, block,
+            ps.at[2, s * outer + m], pr.at[2, s * outer + m], wire.to_low(),
         )
 
     def fold_low(r, mask):
@@ -507,6 +539,10 @@
     for step in range(1, experts):
         over_expert(experts - step).start()
     own.wait()
+    own_features.wait()
+    for s in range(1, sections):
+        plane_side(s, 0).start()
+    plane_low(0, 0).start()
 
     def mask_of(position):
         return lax.rem(experts - position, experts)
@@ -552,6 +588,26 @@
                 over_high(m, now).wait_recv()
                 over_low(m, now).start()
 
+        @pl.when(step == 0)
+        def _():
+            for m in range(1, outer):
+                plane_high(m).start()
+
+        @pl.when(step == 1)
+        def _():
+            for m in range(1, outer):
+                plane_high(m).wait_recv()
+                for s in range(1, sections):
+                    plane_side(s, m).start()
+                plane_low(0, m).start()
+
+        @pl.when(step == 2)
+        def _():
+            for s in range(1, sections):
+                for m in range(outer):
+                    plane_side(s, m).wait_recv()
+                    plane_low(s, m).start()
+
         @pl.when(leaving)
         def _():
             fold_high(0, last, step - 2)
@@ -567,6 +623,13 @@
         def _():
             fold_high(1, last, step - 2)
 
+    for m in range(1, outer):
+        plane_high(m).wait_send()
+    for s in range(sections):
+        for m in range(outer):
+            if s:
+                plane_side(s, m).wait_send()
+            plane_low(s, m).wait()
     for mask in range(experts):
         for r in range(2):
             if mask:
@@ -583,7 +646,7 @@
             over_low(m, mask).wait_send()
 
 
-def run_experts(sizes, ident, rows, grads, gate_weight, up_weight, down_weight):
+def run_experts(sizes, ident, rows, grads, features, gate_weight, up_weight, down_weight):
     sections, experts, ways = sizes
     outer = ways // 2
     span = max(outer - 1, 1)
@@ -600,13 +663,15 @@
         (2, outer, experts),
         (2, span, experts),
         (2, experts),
+        (3, sections * outer),
     ):
         sems += [pltpu.SemaphoreType.DMA(shape)] * 2
     return pl.pallas_call(
         functools.partial(expert_kernel, sizes),
-        out_shape=[jax.ShapeDtypeStruct(buckets, jnp.bfloat16)] * 2,
-        in_specs=[WHOLE, WHOLE, anywhere, anywhere, anywhere],
-        out_specs=[WHOLE, WHOLE],
+        out_shape=[jax.ShapeDtypeStruct(buckets, jnp.bfloat16)] * 2
+        + [jax.ShapeDtypeStruct((ways * sections,) + features.shape, jnp.bfloat16)],
+        in_specs=[WHOLE, WHOLE, WHOLE, anywhere, anywhere, anywhere],
+        out_specs=[WHOLE, WHOLE, WHOLE],
         scratch_shapes=[
             low(ways, *buckets),
             low(*gate_weight.shape[1:]),
@@ -621,11 +686,11 @@
             low(2, *buckets),
         ]
         + sems
-        + [pltpu.SemaphoreType.DMA((3,)), pltpu.SemaphoreType.DMA],
+        + [pltpu.SemaphoreType.DMA((3,)), pltpu.SemaphoreType.DMA((2,))],
         compiler_params=pltpu.CompilerParams(
             collective_id=ident, has_side_effects=True, vmem_limit_bytes=62 * 1024 * 1024
         ),
-    )(rows, grads, gate_weight, up_weight, down_weight)
+    )(rows, grads, features, gate_weight, up_weight, down_weight)
 
 
 def shards(
@@ -664,12 +729,12 @@
     spread_shape = (data_ways,) + buckets
     grad_buffer = jnp.dot(placing, out_grad).reshape(buckets)
     weight_rows = out_weight.shape[0]
-    quarter = 2 * sections
+    quarter = data_ways * sections
     keys_all, values_all, full_out, grad_gathered = call(
         opening_kernel,
         sizes,
         0,
-        4 * outer + experts * (1 + 2 * outer) + experts * (2 + 2 * sections),
+        4 * outer + experts * (1 + 2 * outer) + experts * (2 + 2 * data_ways * sections),
         (
             attn_keys,
             attn_values,
@@ -708,8 +773,8 @@
     unit_rows = hidden * inv_rms
     normed = (unit_rows * norm_gain).astype(jnp.bfloat16)
     send_buffer = jnp.dot(placing, normed).reshape(buckets)
-    grad_returned, returned = run_experts(
-        sizes, 1, send_buffer, grad_gathered, gate_weight, up_weight, down_weight
+    grad_returned, returned, features_all = run_experts(
+        sizes, 1, send_buffer, grad_gathered, attended.T, gate_weight, up_weight, down_weight
     )
     expert_back = contract_first(placing, returned.reshape(experts * capacity, D))
     layer_out = (hidden + expert_back.astype(jnp.float32)).astype(jnp.bfloat16)
@@ -721,12 +786,7 @@
     ).astype(jnp.bfloat16)
     ways = data_ways * sections
     width = D // ways
-    products = jnp.einsum(
-        "ta,tpc->pac",
-        attended,
-        resid_grad.reshape(tokens_here, ways, width),
-        preferred_element_type=jnp.float32,
-    ).astype(jnp.bfloat16)
+    columns = resid_grad.reshape(tokens_here, ways, width).transpose(1, 0, 2)
     grad_attended = contract_last(resid_grad, full_out).astype(jnp.bfloat16)
     grad_heads = grad_attended.reshape(tokens_here, HEADS, HEAD)
     grad_probs = jnp.einsum(
@@ -762,18 +822,21 @@
         closing_kernel,
         sizes,
         2,
-        4 * outer + experts * (1 + sections + outer + 1) + 3 * ways,
-        (pair_parts, products.reshape(ways, experts, weight_rows, width)),
+        4 * outer + experts + 4 * ways,
+        (
+            pair_parts,
+            features_all.reshape(ways, experts, weight_rows, tokens_here),
+            columns,
+        ),
         (pair, (ways,) + block),
         (
             (outer,) + pair,
             (max(outer - 1, 1),) + pair,
-            (experts, outer * sections) + block,
-            (max(sections - 1, 1), experts, outer) + block,
-            (max(outer - 1, 1), experts) + block,
+            columns.shape,
             (experts,) + block,
             (experts - 1,) + block,
         ),
+        extra=(pltpu.SemaphoreType.DMA,),
     )
     key_grad, value_grad = key_value[0], key_value[1]
     weight_grad = weight_parts.transpose(1, 0, 2).reshape(weight_rows, D).astype(jnp.float32)

time: 303 us -> 267 us (0.88)
  Pallas kernels: 244 us -> 217 us
  local copies, waits for them, and re-layouts: 26.1 us -> 21.7 us
  matrix products: 25 us -> 21.7 us
    pallas_call x2, Pallas kernels: 124 us -> 97.4 us  [call(): pl.pallas_call(functools.partial(kernel, sizes), out_shape=[low(s) for s...]
    convert_element_type x1, local copies, waits for them, and re-layouts: 6.47 us -> 1.01 us  [shards(): resid_grad = (out_grad.astype(jnp.float32) + inv_rms * (scaled - unit_row...]
    dot_general x1 -> x0, matrix products: 3.22 us -> none  [shards(): jnp.einsum('ta,tpc->pac', attended, resid_grad.reshape(tokens_here, ways,...]
    unnamed x36 -> x34, local copies, waits for them, and re-layouts: 9.14 us -> 9.21 us
where the time goes in v3:
time: 267 us
  Pallas kernels  217 us (81%)
  local copies, waits for them, and re-layouts  21.7 us (8%)
  matrix products  21.7 us (8%)
  other arithmetic  5 us (2%)
    pallas_call x1, Pallas kernels, run_experts(): pl.pallas_call(functools.partial(expert_kernel, sizes), out_shape=[jax.Sh...  120 us
    pallas_call x2, Pallas kernels, call(): pl.pallas_call(functools.partial(kernel, sizes), out_shape=[low(s) for s...  97.4 us
    unnamed x34, local copies, waits for them, and re-layouts  9.21 us

profile of v3, /device:TPU:0, one launch (start us, length us, event | category | flops | bytes accessed | tf_op | source)
XLA Modules:
  0.0 266.5 jit_solution(14686378934706504998)
XLA Ops:
  0.6 0.0 copy-start
  0.6 0.9 fusion.10
  1.5 0.7 convert_add_fusion
  2.2 2.4 fusion.25
  4.6 62.2 %shard_map.154 = (bf16[4,128,1024]{2,1,0:T(8,128)(2,1)}, bf16[4,128,1024]{2,1,0:T(8,128)(2,1)}, bf16[4,8,32,2048]{3,2,1,0:T(8,128)(2,1)}, bf16[4,4,64,2048]{3,2,1,0:T(8,128)(2,1)}) custom-call(bf16[128,1024]{1,0:T(8,128)(2,1)} %keys.1, bf16[128,1024]{1,0:T(8,128)(2,1)} %values.1, bf16[8,32,2048]{2,1,0:T(8,128)(2,1)} %bitcast.103, bf16[4,64,2048]{2,1,0:T(8,128)(2,1)} %bitcast.95), custom_call_target="tpu_custom_call" | custom-call | tf_op jit(solution)/shard_map/pallas_call | solution.py:358
  66.9 2.6 copy.60
  69.5 0.3 copy.61
  69.8 0.7 copy.41
  70.5 0.0 copy-done
  70.5 0.0 copy-start.2
  70.5 0.5 fusion.21
  71.0 0.0 copy-start.5
  71.0 2.0 fusion.41
  73.0 2.3 convolution_convert_fusion.1
  75.4 0.0 copy-start.9
  75.4 0.0 copy-start.14
  75.4 3.2 %multiply_reduce_fusion.2 = (f32[128]{0:T(128)S(1)}, f32[128,2048]{1,0:T(8,128)S(1)}) fusion(bf16[128,1024]{0,1:T(8,128)(2,1)S(1)} %bitcast.100, bf16[1024,2048]{1,0:T(8,128)(2,1)} %bitcast.91, bf16[128,2048]{1,0:T(8,128)(2,1)} %param.11), kind=kOutput, calls=%fused_computation.27 | convolution fusion | flops 537919360 | bytes 6029824 | tf_op jit(solution)/shard_map/dot_general | solution.py:769
  78.6 0.0 copy-done.9
  78.7 1.5 fusion.15
  80.2 119.9 %shard_map.155 = (bf16[4,64,2048]{2,1,0:T(8,128)(2,1)}, bf16[4,64,2048]{2,1,0:T(8,128)(2,1)}, bf16[8,1024,128]{2,1,0:T(8,128)(2,1)}) custom-call(bf16[4,64,2048]{2,1,0:T(8,128)(2,1)} %bitcast.94, bf16[4,4,64,2048]{3,2,1,0:T(8,128)(2,1)} %get-tuple-element.18.grads, bf16[1024,128]{1,0:T(8,128)(2,1)} %bitcast.101, bf16[1,2048,1024]{2,1,0:T(8,128)(2,1)} %gate_hbm.1, ...), custom_call_target="tpu_custom_call" | custom-call | tf_op jit(solution)/shard_map/pallas_call | solution.py:669
  200.0 0.0 copy-start.12
  200.1 2.5 fusion.1
  202.5 0.4 multiply_reduce_fusion.1
  203.0 0.6 copy-done.8
  203.6 0.3 add_convert_fusion
  203.9 1.0 copy-done.1
  204.9 1.5 convolution_convert_fusion.2
  206.4 0.2 copy.58
  206.6 3.2 %fusion.7 = bf16[512,8,128]{0,2,1:T(8,128)(2,1)S(1)} fusion(bf16[128,8,128]{0,2,1:T(8,128)(2,1)S(1)} %bitcast.110, f32[8,128]{1,0:T(8,128)S(1)} %get-tuple-element.38, f32[8,512,128]{2,1,0:T(8,128)} %copy-done.5), kind=kOutput, calls=%fused_computation.16 | convolution fusion | flops 137364992 | bytes 3411968 | tf_op jit(solution)/shard_map/hts,thd->shd/dot_general | solution.py:809
  209.8 1.1 reshape.94
  210.9 2.6 copy.57
  213.5 1.0 copy.48
  214.5 2.0 copy.49
  216.5 1.7 multiply_reduce_fusion
  218.2 0.3 multiply_convert_fusion.1
  218.5 0.9 copy-done.3
  219.4 1.1 fusion.9
  220.6 0.4 fusion.8
  221.0 0.7 copy.44
  221.7 0.5 stack_reshape.8
  222.2 0.0 copy-done.7
  222.2 1.5 pad_maximum_fusion.parts
  223.7 35.1 %shard_map.156 = (bf16[2,128,1024]{2,1,0:T(8,128)(2,1)}, bf16[8,256,256]{2,1,0:T(8,128)(2,1)}) custom-call(bf16[4,2,128,1024]{3,2,1,0:T(8,128)(2,1)} %pad_maximum_fusion.parts, bf16[8,4,256,128]{3,2,1,0:T(8,128)(2,1)} %bitcast.98, bf16[8,128,256]{2,1,0:T(8,128)(2,1)} %bitcast.97), custom_call_target="tpu_custom_call" | custom-call | tf_op jit(solution)/shard_map/pallas_call | solution.py:358
  258.9 0.9 copy.51
  259.7 1.9 slice_bitcast_fusion
  261.6 0.2 convert_bitcast_fusion
  261.8 1.9 copy.50
  263.7 2.9 %copy.52 = f32[256,2048]{1,0:T(8,128)} copy(f32[256,2048]{0,1:T(8,128)} %bitcast.93) | data formatting | bytes 4194304
  (20 shorter events, 0.0 us)
Async XLA Ops:
  0.6 69.9 %copy-start = (bf16[128,1024]{1,0:T(8,128)(2,1)S(1)}, bf16[128,1024]{1,0:T(8,128)(2,1)}, u32[]{:S(2)}) copy-start(bf16[128,1024]{1,0:T(8,128)(2,1)} %param.12) | copy-start | bytes 786436
  66.9 2.7 copy-start.13
  70.5 2.5 copy-start.2
  71.0 2.0 copy-start.5
  75.4 3.2 %copy-start.9 = (bf16[8,128,128]{2,1,0:T(8,128)(2,1)}, bf16[8,128,128]{2,1,0:T(8,128)(2,1)S(1)}, u32[]{:S(2)}) copy-start(bf16[8,128,128]{2,1,0:T(8,128)(2,1)S(1)} %convolution_convert_fusion.1) | copy-start | bytes 786436
  75.4 3.3 %copy-start.14 = (f32[2048]{0:T(1024)S(1)}, f32[2048]{0:T(1024)}, u32[]{:S(2)}) copy-start(f32[2048]{0:T(1024)} %param.16) | copy-start | bytes 24580
  200.0 2.5 copy-start.12
  202.5 1.0 copy-start.8
  202.5 2.4 copy-start.1
  204.9 8.6 %copy-start.6 = (bf16[128,2048]{1,0:T(8,128)(2,1)}, bf16[128,2048]{1,0:T(8,128)(2,1)S(1)}, u32[]{:S(2)}) copy-start(bf16[128,2048]{1,0:T(8,128)(2,1)S(1)} %add_convert_fusion) | copy-start | bytes 1572868
  210.9 5.6 %copy-start.4 = (f32[8,128,512]{1,2,0:T(8,128)S(1)}, f32[8,128,512]{1,2,0:T(8,128)}, u32[]{:S(2)}) copy-start(f32[8,128,512]{1,2,0:T(8,128)} %get-tuple-element.39) | copy-start | bytes 6291460
  218.2 1.2 copy-start.3
  221.0 1.2 copy-start.7
  223.7 35.2 %copy-start.11 = (bf16[8,128,128]{2,1,0:T(8,128)(2,1)S(1)}, bf16[8,128,128]{2,1,0:T(8,128)(2,1)}, u32[]{:S(2)}) copy-start(bf16[8,128,128]{2,1,0:T(8,128)(2,1)} %fusion.9) | copy-start | bytes 786436
  258.9 2.7 %copy-start.10 = (bf16[8,256,256]{2,1,0:T(8,128)(2,1)S(1)}, bf16[8,256,256]{2,1,0:T(8,128)(2,1)}, u32[]{:S(2)}) copy-start(bf16[8,256,256]{2,1,0:T(8,128)(2,1)} %get-tuple-element.23) | copy-start | bytes 3145732

commit v4 on v3

--- a/solution.py
+++ b/solution.py
@@ -552,6 +552,23 @@
         incoming, current, leaving = step < experts, step >= 1, step >= 2
         now, before, last = mask_of(step), mask_of(step - 1), mask_of(step - 2)
 
+        @pl.when(leaving)
+        def _():
+            fold_low(1, last)
+
+        @pl.when(step == 1)
+        def _():
+            for load in loads:
+                load.wait()
+
+        busy = current & (step <= experts)
+
+        @pl.when(busy)
+        def _():
+            for m in range(outer):
+                over_low(m, before).wait_recv()
+            units(before)
+
         @pl.when(incoming)
         def _():
             @pl.when(step > 0)
@@ -562,22 +579,8 @@
                 over_high(m, now).start()
             over_low(0, now).start()
 
-        @pl.when(leaving)
-        def _():
-            fold_low(1, last)
-
-        @pl.when(step == 1)
-        def _():
-            for load in loads:
-                load.wait()
-
-        busy = current & (step <= experts)
-
         @pl.when(busy)
         def _():
-            for m in range(outer):
-                over_low(m, before).wait_recv()
-            units(before)
             grad_products(before)
             for h in range(outer):
                 back_low(0, h, before).start()

time: 267 us -> 273 us (1.022)
  Pallas kernels: 217 us -> 223 us
    pallas_call x1, Pallas kernels: 120 us -> 127 us  [run_experts(): pl.pallas_call(functools.partial(expert_kernel, sizes), out_shape=[jax.Sh...]
where the time goes in v4:
time: 273 us; the launch traced here: 272 us
  Pallas kernels  223 us (82%)
  local copies, waits for them, and re-layouts  21.7 us (8%)
  matrix products  21.7 us (8%)
  other arithmetic  5 us (2%)
    pallas_call x1, Pallas kernels, run_experts(): pl.pallas_call(functools.partial(expert_kernel, sizes), out_shape=[jax.Sh...  127 us
    pallas_call x2, Pallas kernels, call(): pl.pallas_call(functools.partial(kernel, sizes), out_shape=[low(s) for s...  95.8 us
    unnamed x34, local copies, waits for them, and re-layouts  9.21 us

profile of v4, /device:TPU:0, one launch (start us, length us, event | category | flops | bytes accessed | tf_op | source)
XLA Modules:
  0.0 272.2 jit_solution(16496600137680035412)
XLA Ops:
  0.6 0.0 copy-start
  0.6 0.9 fusion.10
  1.5 0.7 convert_add_fusion
  2.2 2.4 fusion.25
  4.6 62.2 %shard_map.154 = (bf16[4,128,1024]{2,1,0:T(8,128)(2,1)}, bf16[4,128,1024]{2,1,0:T(8,128)(2,1)}, bf16[4,8,32,2048]{3,2,1,0:T(8,128)(2,1)}, bf16[4,4,64,2048]{3,2,1,0:T(8,128)(2,1)}) custom-call(bf16[128,1024]{1,0:T(8,128)(2,1)} %keys.1, bf16[128,1024]{1,0:T(8,128)(2,1)} %values.1, bf16[8,32,2048]{2,1,0:T(8,128)(2,1)} %bitcast.103, bf16[4,64,2048]{2,1,0:T(8,128)(2,1)} %bitcast.95), custom_call_target="tpu_custom_call" | custom-call | tf_op jit(solution)/shard_map/pallas_call | solution.py:358
  66.9 0.0 copy-start.13
  66.9 2.6 copy.60
  69.5 0.0 copy-done.13
  69.5 0.3 copy.61
  69.8 0.7 copy.41
  70.5 0.5 fusion.21
  71.0 2.0 fusion.41
  73.0 0.0 copy-done.5
  73.0 2.3 convolution_convert_fusion.1
  75.4 0.0 copy-start.9
  75.4 0.0 copy-start.14
  75.4 3.2 %multiply_reduce_fusion.2 = (f32[128]{0:T(128)S(1)}, f32[128,2048]{1,0:T(8,128)S(1)}) fusion(bf16[128,1024]{0,1:T(8,128)(2,1)S(1)} %bitcast.100, bf16[1024,2048]{1,0:T(8,128)(2,1)} %bitcast.91, bf16[128,2048]{1,0:T(8,128)(2,1)} %param.11), kind=kOutput, calls=%fused_computation.27 | convolution fusion | flops 537919360 | bytes 6029824 | tf_op jit(solution)/shard_map/dot_general | solution.py:772
  78.7 0.0 copy-done.14
  78.7 1.5 fusion.15
  80.2 127.1 %shard_map.155 = (bf16[4,64,2048]{2,1,0:T(8,128)(2,1)}, bf16[4,64,2048]{2,1,0:T(8,128)(2,1)}, bf16[8,1024,128]{2,1,0:T(8,128)(2,1)}) custom-call(bf16[4,64,2048]{2,1,0:T(8,128)(2,1)} %bitcast.94, bf16[4,4,64,2048]{3,2,1,0:T(8,128)(2,1)} %get-tuple-element.18.grads, bf16[1024,128]{1,0:T(8,128)(2,1)} %bitcast.101, bf16[1,2048,1024]{2,1,0:T(8,128)(2,1)} %gate_hbm.1, ...), custom_call_target="tpu_custom_call" | custom-call | tf_op jit(solution)/shard_map/pallas_call | solution.py:672
  207.3 2.5 fusion.1
  209.8 0.4 multiply_reduce_fusion.1
  210.2 0.6 copy-done.8
  210.8 0.3 add_convert_fusion
  211.1 1.0 copy-done.1
  212.1 1.5 convolution_convert_fusion.2
  213.6 0.2 copy.58
  213.8 3.2 %fusion.7 = bf16[512,8,128]{0,2,1:T(8,128)(2,1)S(1)} fusion(bf16[128,8,128]{0,2,1:T(8,128)(2,1)S(1)} %bitcast.110, f32[8,128]{1,0:T(8,128)S(1)} %get-tuple-element.38, f32[8,512,128]{2,1,0:T(8,128)} %copy-done.5), kind=kOutput, calls=%fused_computation.16 | convolution fusion | flops 137364992 | bytes 3411968 | tf_op jit(solution)/shard_map/hts,thd->shd/dot_general | solution.py:812
  217.0 1.1 reshape.94
  218.1 2.6 copy.57
  220.7 1.0 copy.48
  221.7 2.0 copy.49
  223.8 1.7 multiply_reduce_fusion
  225.4 0.0 copy-start.3
  225.5 0.3 multiply_convert_fusion.1
  225.8 0.9 copy-done.3
  226.7 1.1 fusion.9
  227.8 0.4 fusion.8
  228.2 0.7 copy.44
  228.9 0.5 stack_reshape.8
  229.4 0.0 copy-done.7
  229.5 1.5 pad_maximum_fusion.parts
  231.0 33.6 %shard_map.156 = (bf16[2,128,1024]{2,1,0:T(8,128)(2,1)}, bf16[8,256,256]{2,1,0:T(8,128)(2,1)}) custom-call(bf16[4,2,128,1024]{3,2,1,0:T(8,128)(2,1)} %pad_maximum_fusion.parts, bf16[8,4,256,128]{3,2,1,0:T(8,128)(2,1)} %bitcast.98, bf16[8,128,256]{2,1,0:T(8,128)(2,1)} %bitcast.97), custom_call_target="tpu_custom_call" | custom-call | tf_op jit(solution)/shard_map/pallas_call | solution.py:358
  264.6 0.9 copy.51
  265.4 1.9 slice_bitcast_fusion
  267.3 0.2 convert_bitcast_fusion
  267.5 1.9 copy.50
  269.4 2.9 %copy.52 = f32[256,2048]{1,0:T(8,128)} copy(f32[256,2048]{0,1:T(8,128)} %bitcast.93) | data formatting | bytes 4194304
  (20 shorter events, 0.0 us)
Async XLA Ops:
  0.6 69.9 %copy-start = (bf16[128,1024]{1,0:T(8,128)(2,1)S(1)}, bf16[128,1024]{1,0:T(8,128)(2,1)}, u32[]{:S(2)}) copy-start(bf16[128,1024]{1,0:T(8,128)(2,1)} %param.12) | copy-start | bytes 786436
  66.9 2.7 copy-start.13
  70.5 2.5 copy-start.2
  71.0 2.0 copy-start.5
  75.4 3.2 %copy-start.9 = (bf16[8,128,128]{2,1,0:T(8,128)(2,1)}, bf16[8,128,128]{2,1,0:T(8,128)(2,1)S(1)}, u32[]{:S(2)}) copy-start(bf16[8,128,128]{2,1,0:T(8,128)(2,1)S(1)} %convolution_convert_fusion.1) | copy-start | bytes 786436
  75.4 3.3 %copy-start.14 = (f32[2048]{0:T(1024)S(1)}, f32[2048]{0:T(1024)}, u32[]{:S(2)}) copy-start(f32[2048]{0:T(1024)} %param.16) | copy-start | bytes 24580
  207.3 2.5 copy-start.12
  209.8 1.0 copy-start.8
  209.8 2.4 copy-start.1
  212.1 8.6 %copy-start.6 = (bf16[128,2048]{1,0:T(8,128)(2,1)}, bf16[128,2048]{1,0:T(8,128)(2,1)S(1)}, u32[]{:S(2)}) copy-start(bf16[128,2048]{1,0:T(8,128)(2,1)S(1)} %add_convert_fusion) | copy-start | bytes 1572868
  218.1 5.6 %copy-start.4 = (f32[8,128,512]{1,2,0:T(8,128)S(1)}, f32[8,128,512]{1,2,0:T(8,128)}, u32[]{:S(2)}) copy-start(f32[8,128,512]{1,2,0:T(8,128)} %get-tuple-element.39) | copy-start | bytes 6291460
  225.4 1.2 copy-start.3
  228.2 1.2 copy-start.7
  231.0 33.6 %copy-start.11 = (bf16[8,128,128]{2,1,0:T(8,128)(2,1)S(1)}, bf16[8,128,128]{2,1,0:T(8,128)(2,1)}, u32[]{:S(2)}) copy-start(bf16[8,128,128]{2,1,0:T(8,128)(2,1)} %fusion.9) | copy-start | bytes 786436
  264.6 2.7 %copy-start.10 = (bf16[8,256,256]{2,1,0:T(8,128)(2,1)S(1)}, bf16[8,256,256]{2,1,0:T(8,128)(2,1)}, u32[]{:S(2)}) copy-start(bf16[8,256,256]{2,1,0:T(8,128)(2,1)} %get-tuple-element.23) | copy-start | bytes 3145732
